TPU v7x, 256 devices: a whole 4x4x8 slice. The times are simulated.
256 devices in a mesh: rep: 16 (over y, x_hi, core), fsdp: 16 (over z, x_lo).
Axes of the slice: x: 4 (x_hi: 2, x_lo: 2; x = x_hi * 2 + x_lo), y: 4, z: 8, core: 2. Of those that a mesh axis runs over, the one named last changes fastest.
Arguments:
- activations: bfloat16 [16, 6144, 4096], P('rep', 'fsdp'), may hold values from -6 to 6
- kv_weight: bfloat16 [16, 4096, 1024], P('rep', 'fsdp'), may hold values from -0.09375 to 0.09375
- kv_cotangent: bfloat16 [16, 6144, 1024], P('rep', 'fsdp'), may hold values from -6 to 6
- first_moment: float32 [16, 4096, 1024], P('rep', 'fsdp'), may hold values from -48 to 48
- second_moment: float32 [16, 4096, 1024], P('rep', 'fsdp'), may hold values from 10 to 1000
- partner: int32 [16], replicated, may hold values from 0 to 15, as said below
- mix_numerator: int32 [16], replicated, may hold values from 8 to 56
Outputs:
- kv_out: bfloat16 [16, 6144, 1024], P('rep', 'fsdp')
- x_grad: bfloat16 [16, 6144, 4096], P('rep', 'fsdp')
- new_weight: bfloat16 [16, 4096, 1024], P('rep', 'fsdp')
- new_first: float32 [16, 4096, 1024], P('rep', 'fsdp')
- new_second: float32 [16, 4096, 1024], P('rep', 'fsdp')
Inputs may be any that keep to these rules, and one draw needn't show every extreme that they name: partner[partner[r]] == r and partner[r] != r for every replica r.
All inputs are finite; a program needn't handle non-finite values.
Results may differ from a plain program's by a relative error of at most 0.018.
Values may be sent and summed in bfloat16 or wider, within the bound.
A program may use at most 128 MiB of HBM per device.

v0:
```python
import jax
import jax.numpy as jnp
from jax import lax
from jax.sharding import PartitionSpec as P

beta_one = 0.9
beta_two = 0.999
learn_rate = 0.02
weight_decay = 0.1
adam_eps = 1e-08
corr_one = 1.0 - beta_one**10
corr_two = 1.0 - beta_two**10
mix_denom = 64.0


def per_device(
    activations, kv_weight, kv_cotangent, first_moment, second_moment, partner, mix_numerator
):
    tokens_in = activations[0]
    cotangent = kv_cotangent[0]
    weights = kv_weight[0]
    piece = lax.all_gather(weights, "fsdp", axis=0, tiled=True)
    block = tokens_in
    forward = jnp.dot(block, piece, preferred_element_type=jnp.float32)
    partial_back = jnp.einsum("tc,rc->tr", cotangent, piece, preferred_element_type=jnp.float32)
    backward = partial_back
    forward, backward = (forward, backward)
    keys_values = forward.astype(jnp.bfloat16)
    input_grad = backward.astype(jnp.bfloat16)
    block = tokens_in
    gradient = lax.psum_scatter(
        jnp.einsum("td,tc->dc", block, cotangent, preferred_element_type=jnp.float32).astype(
            jnp.bfloat16
        ),
        "fsdp",
        scatter_dimension=0,
        tiled=True,
    ).astype(jnp.float32)
    moment_new_a = beta_one * first_moment[0] + (1.0 - beta_one) * gradient
    moment_new_b = beta_two * second_moment[0] + (1.0 - beta_two) * gradient * gradient
    old_weight = weights.astype(jnp.float32)
    update = (
        moment_new_a / corr_one / (jnp.sqrt(moment_new_b / corr_two) + adam_eps)
        + weight_decay * old_weight
    )
    stepped = (old_weight - learn_rate * update).astype(jnp.bfloat16)
    replica = lax.axis_index("rep")
    partner_index = partner[replica]
    mixing = mix_numerator[replica].astype(jnp.float32) / mix_denom
    piece = lax.all_gather(stepped[None], "rep", axis=0, tiled=True)
    count = piece.shape[0]
    matching = jnp.arange(count, dtype=jnp.int32) == partner_index
    chosen = jnp.sum(jnp.where(matching[:, None, None], piece, jnp.zeros_like(piece)), axis=0)
    averaged = (
        (1.0 - mixing) * stepped.astype(jnp.float32) + mixing * chosen.astype(jnp.float32)
    ).astype(jnp.bfloat16)
    return (
        keys_values[None],
        input_grad[None],
        averaged[None],
        moment_new_a[None],
        moment_new_b[None],
    )


def solution(mesh):
    placed = (
        P("rep", "fsdp", None),
        P("rep", "fsdp", None),
        P("rep", "fsdp", None),
        P("rep", "fsdp", None),
        P("rep", "fsdp", None),
        P(),
        P(),
    )
    return jax.shard_map(
        per_device,
        mesh=mesh,
        in_specs=placed,
        out_specs=(
            P("rep", "fsdp", None),
            P("rep", "fsdp", None),
            P("rep", "fsdp", None),
            P("rep", "fsdp", None),
            P("rep", "fsdp", None),
        ),
        check_vma=False,
    )
```

profile of v0, /device:TPU:1, one launch (start us, length us, event | category | flops | bytes accessed | tf_op | source)
XLA Modules:
  0.0 484.9 jit_solution(2091200322938265328)
XLA Ops:
  7.2 0.0 copy-start
  7.2 0.0 reduce-scatter.2.cloned.1.call-start
  7.2 1.8 copy-done
  9.1 7.8 %convolution_convert_fusion = bf16[4096,1024]{1,0:T(8,128)(2,1)} fusion(bf16[1,384,4096]{2,1,0:T(8,128)(2,1)S(1)} %copy-done, bf16[1,384,1024]{2,1,0:T(8,128)(2,1)} %param.9), kind=kOutput, calls=%fused_computation.5 | convolution fusion | flops 3225419776 | bytes 12320768 | tf_op jit(solution)/shard_map/td,tc->dc/dot_general | solution.py:32
  16.9 0.0 reduce-scatter.2.cloned.1.call-update
  16.9 0.0 all-gather.5.cloned.1.call-start
  17.0 0.7 all-gather.5.cloned.1.call-update
  17.7 0.0 all-gather.7.cloned.1.call-start
  17.7 185.9 %reduce-scatter.2.cloned.1.call-done = bf16[256,1024]{1,0:T(8,128)(2,1)} async-done(((bf16[4096,1024]{1,0:T(8,128)(2,1)}), bf16[256,1024]{1,0:T(8,128)(2,1)}) %reduce-scatter.2.cloned.1.call-update) | async-done | bytes 524304 | tf_op jit(solution)/shard_map/reduce_scatter | solution.py:31
  203.6 4.2 fusion.30
  207.8 0.0 all-gather.7.cloned.1.call-update
  207.8 0.0 copy-done.3
  207.8 0.6 dynamic_slice.7
  208.4 0.0 copy-done.4
  208.4 0.6 dynamic_slice.6
  209.7 0.7 iota_compare_fusion
  210.3 178.4 %all-gather.5.cloned.1.call-done = bf16[1,4096,1024]{2,1,0:T(8,128)(2,1)} async-done(((bf16[1,256,1024]{2,1,0:T(8,128)(2,1)}), bf16[1,4096,1024]{2,1,0:T(8,128)(2,1)}) %all-gather.5.cloned.1.call-update) | async-done | bytes 8388624 | tf_op jit(solution)/shard_map/all_gather | solution.py:22
  388.7 8.9 %fusion.7 = bf16[1,384,4096]{2,1,0:T(8,128)(2,1)} fusion(bf16[1,4096,1024]{2,1,0:T(8,128)(2,1)} %all-gather.5.cloned.1.call-done, bf16[1,384,1024]{2,1,0:T(8,128)(2,1)} %param.9), kind=kOutput, calls=%fused_computation.7 | convolution fusion | flops 3222798336 | bytes 12320768 | tf_op jit(solution)/shard_map/tc,rc->tr/dot_general | solution.py:25
  397.6 0.0 copy-done.2
  397.6 4.4 fusion.17
  401.9 69.8 %all-gather.7.cloned.1.call-done = bf16[4096,1024]{1,0:T(8,128)(2,1)} async-done(((bf16[256,1024]{1,0:T(8,128)(2,1)}), bf16[4096,1024]{1,0:T(8,128)(2,1)}) %all-gather.7.cloned.1.call-update) | async-done | bytes 8388624 | tf_op jit(solution)/shard_map/all_gather | solution.py:50
  471.7 5.6 %select_reduce_fusion = bf16[256,1024]{1,0:T(8,128)(2,1)S(1)} fusion(bf16[16,256,1024]{2,1,0:T(8,128)(2,1)} %bitcast.55, pred[16]{0:T(512)(128)(4,1)S(1)} %iota_compare_fusion), kind=kLoop, calls=%fused_computation.4 | loop fusion | flops 8126464 | bytes 8912912 | tf_op jit(solution)/shard_map/reduce_sum | solution.py:53
  477.3 0.0 copy-done.1
  477.3 1.0 fusion.31
  (4 shorter events, 0.0 us)
Async XLA Ops:
  7.2 1.9 copy-start
  7.2 196.4 %reduce-scatter.2.cloned.1.call-start = ((), (), s32[]{:S(2)}) async-start(), calls=%async_computation.1 | async-start | bytes 8912896 | tf_op jit(solution)/shard_map/reduce_scatter | solution.py:31
  16.9 190.9 %copy-start.3 = (s32[16]{0:T(128)S(1)}, s32[16]{0:T(128)}, u32[]{:S(2)}) copy-start(s32[16]{0:T(128)} %param.12) | copy-start | bytes 196
  16.9 191.5 %copy-start.4 = (s32[16]{0:T(128)S(1)}, s32[16]{0:T(128)}, u32[]{:S(2)}) copy-start(s32[16]{0:T(128)} %param.13) | copy-start | bytes 196
  16.9 371.8 %all-gather.5.cloned.1.call-start = ((), (), s32[]{:S(2)}) async-start(), calls=%async_computation.2 | async-start | bytes 8912896 | tf_op jit(solution)/shard_map/all_gather | solution.py:22
  17.7 454.0 %all-gather.7.cloned.1.call-start = ((), (), s32[]{:S(2)}) async-start(), calls=%async_computation.3 | async-start | bytes 8912896 | tf_op jit(solution)/shard_map/all_gather | solution.py:50
  388.7 8.9 %copy-start.2 = (bf16[1,4096,1024]{2,1,0:T(8,128)(2,1)S(1)}, bf16[1,4096,1024]{2,1,0:T(8,128)(2,1)}, u32[]{:S(2)}) copy-start(bf16[1,4096,1024]{2,1,0:T(8,128)(2,1)} %all-gather.5.cloned.1.call-done) | copy-start | bytes 25165828
  471.7 5.6 %copy-start.1 = (bf16[256,1024]{1,0:T(8,128)(2,1)S(1)}, bf16[256,1024]{1,0:T(8,128)(2,1)}, u32[]{:S(2)}) copy-start(bf16[256,1024]{1,0:T(8,128)(2,1)} %get-tuple-element.6) | copy-start | bytes 1572868
Sparse Core Ops, SparseCore 0:
  17.0 186.4 reduce-scatter.1
  205.4 183.2 all-gather.4
  392.0 79.6 all-gather.6
where the time goes:
time: 485 us
  waiting for transfers between devices  435 us (90%)
  matrix products  21.1 us (4%)
  between operations  14.4 us (3%)
  other arithmetic  11.5 us (2%)
    reduce_scatter x1, waiting for transfers between devices, per_device(): lax.psum_scatter(jnp.einsum('td,tc->dc', block, cotangent, preferred_elem...  186 us
    all_gather x1, waiting for transfers between devices, per_device(): piece = lax.all_gather(weights, 'fsdp', axis=0, tiled=True)  178 us
    all_gather x1, waiting for transfers between devices, per_device(): piece = lax.all_gather(stepped[None], 'rep', axis=0, tiled=True)  69.8 us
  transfers between devices with their start and end apart: 3, of which 3 were waited for; matrix products, arithmetic and copies ran while one was open for 4% of the time, Pallas kernels for 0%

commit v1 on v0

v1 whole, which is shorter than its diff:
```python
import functools

import jax
import jax.numpy as jnp
from jax import lax
from jax.experimental import pallas as pl
from jax.experimental.pallas import tpu as pltpu
from jax.sharding import PartitionSpec as P

beta_one = 0.9
beta_two = 0.999
learn_rate = 0.02
weight_decay = 0.1
adam_eps = 1e-08
corr_one = 1.0 - beta_one**10
corr_two = 1.0 - beta_two**10
mix_denom = 64.0

MESH = pl.DeviceIdType.MESH
BF = jnp.bfloat16
F32 = jnp.float32
NZ = 8
ORDER = (4, 3, 5, 2, 6, 1, 7, 0)
ROWS_X = 96


def kernel(
    act_h, w_h, cot_h, first_h, second_h, partner_s, mix_s,
    kv_h, xg_h, nw_h, nf_h, ns_h,
    acat, aoth, ccat, wg, kvacc, kvb, xgv, mom, mnew, rs_in, rs_out, gbuf,
    stepped, inbox, outbox, final, nwv,
    load_sem, act_sem, x_send, x_recv, wx_send, wx_recv, ag_send, ag_recv,
    rs_send, rs_recv, ex_send, ex_recv, out_sem, xg_sem,
):
    rep = lax.axis_index("rep")
    me = lax.axis_index("fsdp")
    n_rep = inbox.shape[0]
    tok = cot_h.shape[0]
    rows = w_h.shape[0]
    half = rows // 2
    z, xl = me // 2, me % 2
    up = (rep, lax.rem(z + 1, NZ) * 2 + xl)
    down = (rep, lax.rem(z + NZ - 1, NZ) * 2 + xl)
    side = (rep, z * 2 + 1 - xl)
    ring = (up, down)

    def block_columns(ref, col, slot):
        x = xl if col == 0 else 1 - xl
        index = lax.rem(z + slot, NZ) * 2 + x
        return ref.at[:, pl.ds(pl.multiple_of(index * rows, rows), rows)]

    def remote(src, dst, send, recv, target):
        return pltpu.make_async_remote_copy(
            src_ref=src, dst_ref=dst, send_sem=send, recv_sem=recv,
            device_id=target, device_id_type=MESH,
        )

    loads = {
        "cot": pltpu.make_async_copy(cot_h, ccat.at[pl.ds(0, tok)], load_sem.at[0]),
        "w": pltpu.make_async_copy(w_h, wg.at[0, 0], load_sem.at[1]),
        "first": pltpu.make_async_copy(first_h, mom.at[0], load_sem.at[2]),
        "second": pltpu.make_async_copy(second_h, mom.at[1], load_sem.at[3]),
    }
    for slot in range(NZ):
        loads[0, slot] = pltpu.make_async_copy(
            block_columns(act_h, 0, slot), acat.at[slot, pl.ds(0, tok)], act_sem.at[0, slot]
        )
        loads[1, slot] = pltpu.make_async_copy(
            block_columns(act_h, 1, slot), aoth.at[slot], act_sem.at[1, slot]
        )

    barrier = pltpu.get_barrier_semaphore()
    others = [(lax.rem(rep + k, n_rep), me) for k in range(1, n_rep)]
    for device in (up, down, side, *others):
        pl.semaphore_signal(barrier, inc=1, device_id=device, device_id_type=MESH)
    loads["cot"].start()
    loads["w"].start()
    for slot in (0, 7, 1, 4, 3, 5, 2, 6):
        loads[0, slot].start()
    pl.semaphore_wait(barrier, 3 + n_rep - 1)

    x_copies = {"cot": remote(cot_h, ccat.at[pl.ds(tok, tok)], x_send.at[NZ], x_recv.at[NZ], side)}
    for slot in ORDER:
        x_copies[slot] = remote(
            block_columns(act_h, 1, slot), acat.at[slot, pl.ds(tok, tok)],
            x_send.at[slot], x_recv.at[slot], side,
        )
    wx = [remote(w_h, wg.at[1, 0], wx_send.at[0], wx_recv.at[0], side)]
    for slot in range(1, NZ):
        wx.append(
            remote(
                wg.at[0, slot, pl.ds(0, ROWS_X)], wg.at[1, slot, pl.ds(0, ROWS_X)],
                wx_send.at[slot], wx_recv.at[slot], side,
            )
        )

    def gather(col, direction, hop):
        low, high = (0, rows) if col == 0 else (ROWS_X, rows)
        if hop == NZ // 2:
            middle = (low + high) // 2
            low, high = (low, middle) if direction == 0 else (middle, high)
        if direction == 0:
            src, dst = (NZ - hop + 1) % NZ, NZ - hop
        else:
            src, dst = hop - 1, hop
        span = pl.ds(low, high - low)
        source = w_h.at[span] if (col == 0 and hop == 1) else wg.at[col, src, span]
        return remote(
            source, wg.at[col, dst, span],
            ag_send.at[col, direction, hop - 1], ag_recv.at[col, direction, hop - 1],
            ring[direction],
        )

    ag = {
        (c, d, h): gather(c, d, h) for c in range(2) for d in range(2) for h in range(1, NZ // 2 + 1)
    }

    def gather_start(col, hop):
        for direction in range(2):
            ag[col, direction, hop].start()

    def gather_arrived(col, hop):
        for direction in range(2):
            ag[col, direction, hop].wait_recv()

    xg_copies = []

    def use_block(col, slot, first=False):
        block = wg[col, slot]
        tokens = acat[slot, pl.ds(0, tok)] if col == 0 else aoth[slot]
        term = jnp.dot(tokens, block, preferred_element_type=F32)
        if first:
            kvacc[...] = term
        else:
            kvacc[...] += term
        xgv[col, slot] = lax.dot_general(
            ccat[pl.ds(0, tok)], block, (((1,), (1,)), ((), ())), preferred_element_type=F32
        ).astype(BF)
        copy = pltpu.make_async_copy(
            xgv.at[col, slot], block_columns(xg_h, col, slot), xg_sem.at[col, slot]
        )
        copy.start()
        xg_copies.append(copy)

    def product(slot):
        return lax.dot_general(
            acat[slot], ccat[...], (((0,), (0,)), ((), ())), preferred_element_type=F32
        )

    def reduce_copy(direction, step, part):
        span = pl.ds(part * half, half)
        return remote(
            rs_out.at[direction, step, span], rs_in.at[direction, step, span],
            rs_send.at[direction, step, part], rs_recv.at[direction, step, part],
            ring[direction],
        )

    rs = {(0, 0, 0): reduce_copy(0, 0, 0), (1, 0, 1): reduce_copy(1, 0, 1)}
    for direction in range(2):
        for step in range(1, NZ // 2):
            for part in range(2):
                rs[direction, step, part] = reduce_copy(direction, step, part)

    def reduce_step(step):
        slots = (NZ // 2 - step, NZ // 2 + step)
        for direction in range(2):
            x_copies[slots[direction]].wait_recv()
            gbuf[direction] = product(slots[direction])
        for part in range(2):
            for direction in range(2):
                p = part if step > 1 else (1 - part if direction == 0 else part)
                span = pl.ds(p * half, half)
                value = gbuf[direction, span]
                if (direction, step - 1, p) in rs:
                    rs[direction, step - 1, p].wait_recv()
                    value = value + rs_in[direction, step - 1, span].astype(F32)
                rs_out[direction, step, span] = value.astype(BF)
                rs[direction, step, p].start()

    x_copies["cot"].start()
    gather_start(0, 1)
    for slot in ORDER:
        x_copies[slot].start()
    wx[0].start()
    for slot in range(NZ):
        loads[1, slot].start()
    loads["first"].start()
    loads["second"].start()

    loads["cot"].wait()
    loads["w"].wait()
    for slot in range(NZ):
        loads[0, slot].wait()
    use_block(0, 0, first=True)
    gather_arrived(0, 1)
    gather_start(0, 2)
    wx[7].start()
    wx[1].start()
    use_block(0, 7)
    use_block(0, 1)

    x_copies["cot"].wait_recv()
    x_copies[4].wait_recv()
    gbuf[0] = product(4)
    rs_out[0, 0, pl.ds(0, half)] = gbuf[0, pl.ds(0, half)].astype(BF)
    rs[0, 0, 0].start()
    rs_out[1, 0, pl.ds(half, half)] = gbuf[0, pl.ds(half, half)].astype(BF)
    rs[1, 0, 1].start()

    gather_arrived(0, 2)
    gather_start(0, 3)
    wx[6].start()
    wx[2].start()
    use_block(0, 6)
    use_block(0, 2)

    reduce_step(1)
    reduce_step(2)
    gather_arrived(0, 3)
    gather_start(0, 4)
    wx[5].start()
    wx[3].start()
    reduce_step(3)
    use_block(0, 5)
    use_block(0, 3)
    x_copies[0].wait_recv()
    gbuf[0] = product(0)
    wx[0].wait_recv()
    gather_start(1, 1)
    loads["first"].wait()
    loads["second"].wait()
    for part in range(2):
        span = pl.ds(part * half, half)
        for direction in range(2):
            rs[direction, NZ // 2 - 1, part].wait_recv()
        grad = (
            gbuf[0, span]
            + rs_in[0, NZ // 2 - 1, span].astype(F32)
            + rs_in[1, NZ // 2 - 1, span].astype(F32)
        )
        new_a = beta_one * mom[0, span] + (1.0 - beta_one) * grad
        new_b = beta_two * mom[1, span] + (1.0 - beta_two) * grad * grad
        mnew[0, span] = new_a
        mnew[1, span] = new_b
        old = wg[0, 0, span].astype(F32)
        update = new_a / corr_one / (jnp.sqrt(new_b / corr_two) + adam_eps) + weight_decay * old
        count = n_rep // 2
        stepped[pl.ds(part * count, count)] = (
            (old - learn_rate * update).astype(BF).reshape(count, half // count, old.shape[1])
        )
    outs = [
        pltpu.make_async_copy(mnew.at[0], nf_h, out_sem.at[0]),
        pltpu.make_async_copy(mnew.at[1], ns_h, out_sem.at[1]),
    ]
    for copy in outs:
        copy.start()

    def exchange(phase, k):
        peer = lax.rem(rep + k, n_rep)
        src = (stepped if phase == 0 else outbox).at[peer]
        dst = (inbox if phase == 0 else final).at[rep]
        return remote(src, dst, ex_send.at[phase, k], ex_recv.at[phase, k], (peer, me))

    ex = [[exchange(phase, k) for k in range(1, n_rep)] for phase in range(2)]
    for copy in ex[0]:
        copy.start()
    inbox[rep] = stepped[rep]

    gather_arrived(0, 4)
    wx[4].start()
    gather_arrived(1, 1)
    gather_start(1, 2)
    for copy in ex[0]:
        copy.wait_recv()
    for j in range(n_rep):
        outbox[j] = inbox[partner_s[j]]
    for copy in ex[1]:
        copy.start()
    final[rep] = outbox[rep]

    for slot in range(NZ):
        loads[1, slot].wait()
    use_block(0, 4)
    use_block(1, 0)
    gather_arrived(1, 2)
    gather_start(1, 3)
    for slot in (7, 1, 6, 2):
        wx[slot].wait_recv()
        use_block(1, slot)
    for copy in ex[1]:
        copy.wait_recv()
    mixing = mix_s[rep].astype(F32) / mix_denom
    nwv[...] = (
        (1.0 - mixing) * stepped[...].astype(F32) + mixing * final[...].astype(F32)
    ).astype(BF).reshape(nwv.shape)
    copy = pltpu.make_async_copy(nwv, nw_h, out_sem.at[2])
    copy.start()
    outs.append(copy)
    gather_arrived(1, 3)
    gather_start(1, 4)
    for slot in (5, 3):
        wx[slot].wait_recv()
        use_block(1, slot)
    gather_arrived(1, 4)
    wx[4].wait_recv()
    use_block(1, 4)
    kvb[...] = kvacc[...].astype(BF)
    copy = pltpu.make_async_copy(kvb, kv_h, out_sem.at[3])
    copy.start()
    outs.append(copy)

    for copy in (*x_copies.values(), *wx, *ag.values(), *rs.values(), *ex[0], *ex[1]):
        copy.wait_send()
    for copy in (*outs, *xg_copies):
        copy.wait()


def per_device(
    activations, kv_weight, kv_cotangent, first_moment, second_moment, partner, mix_numerator
):
    act, weights, cot = activations[0], kv_weight[0], kv_cotangent[0]
    tok, width = act.shape
    rows, cols = weights.shape
    n_rep = partner.shape[0]
    dma = pltpu.SemaphoreType.DMA
    hops = NZ // 2
    hbm = pl.BlockSpec(memory_space=pl.ANY)
    smem = pl.BlockSpec(memory_space=pltpu.SMEM)
    outs = pl.pallas_call(
        kernel,
        out_shape=(
            jax.ShapeDtypeStruct((tok, cols), BF),
            jax.ShapeDtypeStruct((tok, width), BF),
            jax.ShapeDtypeStruct((rows, cols), BF),
            jax.ShapeDtypeStruct((rows, cols), F32),
            jax.ShapeDtypeStruct((rows, cols), F32),
        ),
        in_specs=[hbm] * 5 + [smem] * 2,
        out_specs=[hbm] * 5,
        scratch_shapes=[
            pltpu.VMEM((NZ, 2 * tok, rows), BF),
            pltpu.VMEM((NZ, tok, rows), BF),
            pltpu.VMEM((2 * tok, cols), BF),
            pltpu.VMEM((2, NZ, rows, cols), BF),
            pltpu.VMEM((tok, cols), F32),
            pltpu.VMEM((tok, cols), BF),
            pltpu.VMEM((2, NZ, tok, rows), BF),
            pltpu.VMEM((2, rows, cols), F32),
            pltpu.VMEM((2, rows, cols), F32),
            pltpu.VMEM((2, hops, rows, cols), BF),
            pltpu.VMEM((2, hops, rows, cols), BF),
            pltpu.VMEM((2, rows, cols), F32),
            pltpu.VMEM((n_rep, rows // n_rep, cols), BF),
            pltpu.VMEM((n_rep, rows // n_rep, cols), BF),
            pltpu.VMEM((n_rep, rows // n_rep, cols), BF),
            pltpu.VMEM((n_rep, rows // n_rep, cols), BF),
            pltpu.VMEM((rows, cols), BF),
            dma((4,)),
            dma((2, NZ)),
            dma((NZ + 1,)),
            dma((NZ + 1,)),
            dma((NZ,)),
            dma((NZ,)),
            dma((2, 2, hops)),
            dma((2, 2, hops)),
            dma((2, hops, 2)),
            dma((2, hops, 2)),
            dma((2, n_rep)),
            dma((2, n_rep)),
            dma((4,)),
            dma((2, NZ)),
        ],
        name="step",
        compiler_params=pltpu.CompilerParams(
            collective_id=0, has_side_effects=True, vmem_limit_bytes=52 << 20
        ),
    )(act, weights, cot, first_moment[0], second_moment[0], partner, mix_numerator)
    return tuple(out[None] for out in outs)


def solution(mesh):
    split = P("rep", "fsdp", None)
    return jax.shard_map(
        per_device,
        mesh=mesh,
        in_specs=(split,) * 5 + (P(), P()),
        out_specs=(split,) * 5,
        check_vma=False,
    )
```

time: 485 us -> 137 us (0.28)
  waiting for transfers between devices: 435 us -> 0 us
  Pallas kernels: 0 us -> 124 us
  matrix products: 21.1 us -> 0 us
  between operations: 14.4 us -> 0.66 us
  other arithmetic: 11.5 us -> 0 us
  local copies, waits for them, and re-layouts: 3.03 us -> 9.96 us
    all_gather x2 -> x0, waiting for transfers between devices: 248 us -> none  [the longest x1 178 us: per_device(): piece = lax.all_gather(weights, 'fsdp', axis=0, tiled=True)]
    reduce_scatter x1 -> x0, waiting for transfers between devices: 186 us -> none  [per_device(): lax.psum_scatter(jnp.einsum('td,tc->dc', block, cotangent, preferred_elem...]
    pallas_call x0 -> x1, Pallas kernels: none -> 124 us  [per_device(): pl.pallas_call(kernel, out_shape=(jax.ShapeDtypeStruct((tok, cols), BF),...]
    dot_general x3 -> x0, matrix products: 21.1 us -> none  [the longest x1 8.88 us: per_device(): jnp.einsum('tc,rc->tr', cotangent, piece, preferred_element_type=jnp.floa...]
    unnamed x10 -> x15, local copies, waits for them, and re-layouts: 1.86 us -> 9.96 us
    reduce_sum x1 -> x0, other arithmetic: 5.62 us -> none  [per_device(): jnp.sum(jnp.where(matching[:, None, None], piece, jnp.zeros_like(piece)),...]
    broadcast_in_dim x2 -> x0, other arithmetic: 5.21 us -> none  [the longest x1 4.21 us: per_device(): moment_new_b[None]]
  transfers between devices with their start and end apart: 3 -> 0, of which waited for: 3 -> 0; matrix products, arithmetic and copies ran while one was open for 4% -> 0% of each run, Pallas kernels for 0% -> 0%
where the time goes in v1:
time: 137 us; the launch traced here: 134 us
  Pallas kernels  124 us (91%)
  local copies, waits for them, and re-layouts  9.96 us (7%)
    pallas_call x1, Pallas kernels, per_device(): pl.pallas_call(kernel, out_shape=(jax.ShapeDtypeStruct((tok, cols), BF),...  124 us
    unnamed x15, local copies, waits for them, and re-layouts  9.96 us

profile of v1, /device:TPU:1, one launch (start us, length us, event | category | flops | bytes accessed | tf_op | source)
XLA Modules:
  0.0 134.3 jit_solution(9897151864813331422)
XLA Ops:
  0.6 0.0 copy-start
  0.6 1.0 copy-done
  1.7 0.0 copy-start.1
  1.7 0.7 copy-done.1
  2.3 0.0 copy-start.2
  2.3 0.7 copy-done.2
  3.0 123.7 %step.1 = (bf16[384,1024]{1,0:T(8,128)(2,1)S(1)}, bf16[384,4096]{1,0:T(8,128)(2,1)}, bf16[256,1024]{1,0:T(8,128)(2,1)S(1)}, f32[256,1024]{1,0:T(8,128)}, f32[256,1024]{1,0:T(8,128)}) custom-call(bf16[384,4096]{1,0:T(8,128)(2,1)} %bitcast.14, bf16[256,1024]{1,0:T(8,128)(2,1)S(1)} %bitcast.12, bf16[384,1024]{1,0:T(8,128)(2,1)} %bitcast.19, ...), custom_call_target="tpu_custom_call" | custom-call | tf_op jit(solution)/shard_map/step/pallas_call | solution.py:329
  126.7 0.9 copy.17
  127.6 0.0 copy-start.4
  127.6 4.0 %copy.18 = bf16[1,384,4096]{2,1,0:T(8,128)(2,1)} copy(bf16[1,384,4096]{2,1,0:T(8,128)(2,1)} %bitcast.13) | data formatting | bytes 6291456
  131.6 0.0 copy-start.3
  131.6 0.8 copy.19
  132.4 0.0 copy-done.4
  132.4 1.0 copy.20
  133.3 0.0 copy-done.3
  133.3 1.0 copy.21
Async XLA Ops:
  0.6 1.0 copy-start
  1.7 0.7 copy-start.1
  2.3 0.7 copy-start.2
  127.6 4.8 %copy-start.4 = (f32[256,1024]{1,0:T(8,128)S(1)}, f32[256,1024]{1,0:T(8,128)}, u32[]{:S(2)}) copy-start(f32[256,1024]{1,0:T(8,128)} %get-tuple-element.13) | copy-start | bytes 3145732
  131.6 1.8 %copy-start.3 = (f32[256,1024]{1,0:T(8,128)S(1)}, f32[256,1024]{1,0:T(8,128)}, u32[]{:S(2)}) copy-start(f32[256,1024]{1,0:T(8,128)} %get-tuple-element.14) | copy-start | bytes 3145732

commit v2 on v1

--- a/solution.py
+++ b/solution.py
@@ -25,12 +25,12 @@
 
 
 def kernel(
-    act_h, w_h, cot_h, first_h, second_h, partner_s, mix_s,
-    kv_h, xg_h, nw_h, nf_h, ns_h,
-    acat, aoth, ccat, wg, kvacc, kvb, xgv, mom, mnew, rs_in, rs_out, gbuf,
-    stepped, inbox, outbox, final, nwv,
+    act_h, w_h, cot_h, first_h, second_h, partner_h, mix_h,
+    kvb, xgv, nwv, first_new, second_new,
+    acat, aoth, ccat, wg, kvacc, mom, rs_in, rs_out, gbuf,
+    stepped, inbox, outbox, final, scalars,
     load_sem, act_sem, x_send, x_recv, wx_send, wx_recv, ag_send, ag_recv,
-    rs_send, rs_recv, ex_send, ex_recv, out_sem, xg_sem,
+    rs_send, rs_recv, ex_send, ex_recv,
 ):
     rep = lax.axis_index("rep")
     me = lax.axis_index("fsdp")
@@ -60,6 +60,8 @@
         "w": pltpu.make_async_copy(w_h, wg.at[0, 0], load_sem.at[1]),
         "first": pltpu.make_async_copy(first_h, mom.at[0], load_sem.at[2]),
         "second": pltpu.make_async_copy(second_h, mom.at[1], load_sem.at[3]),
+        "partner": pltpu.make_async_copy(partner_h, scalars.at[0], load_sem.at[4]),
+        "mix": pltpu.make_async_copy(mix_h, scalars.at[1], load_sem.at[5]),
     }
     for slot in range(NZ):
         loads[0, slot] = pltpu.make_async_copy(
@@ -123,8 +125,6 @@
         for direction in range(2):
             ag[col, direction, hop].wait_recv()
 
-    xg_copies = []
-
     def use_block(col, slot, first=False):
         block = wg[col, slot]
         tokens = acat[slot, pl.ds(0, tok)] if col == 0 else aoth[slot]
@@ -133,14 +133,10 @@
             kvacc[...] = term
         else:
             kvacc[...] += term
-        xgv[col, slot] = lax.dot_general(
+        x = xl if col == 0 else 1 - xl
+        xgv[lax.rem(z + slot, NZ) * 2 + x] = lax.dot_general(
             ccat[pl.ds(0, tok)], block, (((1,), (1,)), ((), ())), preferred_element_type=F32
         ).astype(BF)
-        copy = pltpu.make_async_copy(
-            xgv.at[col, slot], block_columns(xg_h, col, slot), xg_sem.at[col, slot]
-        )
-        copy.start()
-        xg_copies.append(copy)
 
     def product(slot):
         return lax.dot_general(
@@ -184,8 +180,8 @@
     wx[0].start()
     for slot in range(NZ):
         loads[1, slot].start()
-    loads["first"].start()
-    loads["second"].start()
+    for name in ("first", "second", "partner", "mix"):
+        loads[name].start()
 
     loads["cot"].wait()
     loads["w"].wait()
@@ -240,21 +236,14 @@
         )
         new_a = beta_one * mom[0, span] + (1.0 - beta_one) * grad
         new_b = beta_two * mom[1, span] + (1.0 - beta_two) * grad * grad
-        mnew[0, span] = new_a
-        mnew[1, span] = new_b
+        first_new[span] = new_a
+        second_new[span] = new_b
         old = wg[0, 0, span].astype(F32)
         update = new_a / corr_one / (jnp.sqrt(new_b / corr_two) + adam_eps) + weight_decay * old
         count = n_rep // 2
         stepped[pl.ds(part * count, count)] = (
             (old - learn_rate * update).astype(BF).reshape(count, half // count, old.shape[1])
         )
-    outs = [
-        pltpu.make_async_copy(mnew.at[0], nf_h, out_sem.at[0]),
-        pltpu.make_async_copy(mnew.at[1], ns_h, out_sem.at[1]),
-    ]
-    for copy in outs:
-        copy.start()
-
     def exchange(phase, k):
         peer = lax.rem(rep + k, n_rep)
         src = (stepped if phase == 0 else outbox).at[peer]
@@ -272,8 +261,10 @@
     gather_start(1, 2)
     for copy in ex[0]:
         copy.wait_recv()
+    loads["partner"].wait()
+    loads["mix"].wait()
     for j in range(n_rep):
-        outbox[j] = inbox[partner_s[j]]
+        outbox[j] = inbox[scalars[0, j]]
     for copy in ex[1]:
         copy.start()
     final[rep] = outbox[rep]
@@ -289,13 +280,10 @@
         use_block(1, slot)
     for copy in ex[1]:
         copy.wait_recv()
-    mixing = mix_s[rep].astype(F32) / mix_denom
+    mixing = scalars[1, rep].astype(F32) / mix_denom
     nwv[...] = (
         (1.0 - mixing) * stepped[...].astype(F32) + mixing * final[...].astype(F32)
     ).astype(BF).reshape(nwv.shape)
-    copy = pltpu.make_async_copy(nwv, nw_h, out_sem.at[2])
-    copy.start()
-    outs.append(copy)
     gather_arrived(1, 3)
     gather_start(1, 4)
     for slot in (5, 3):
@@ -305,13 +293,19 @@
     wx[4].wait_recv()
     use_block(1, 4)
     kvb[...] = kvacc[...].astype(BF)
-    copy = pltpu.make_async_copy(kvb, kv_h, out_sem.at[3])
-    copy.start()
-    outs.append(copy)
 
     for copy in (*x_copies.values(), *wx, *ag.values(), *rs.values(), *ex[0], *ex[1]):
         copy.wait_send()
-    for copy in (*outs, *xg_copies):
+
+
+def write_out(kvb, xgv, nwv, first_new, second_new, kv_h, xg_h, nw_h, nf_h, ns_h, sem):
+    rows = xgv.shape[2]
+    pairs = [(xgv.at[i], xg_h.at[:, pl.ds(i * rows, rows)]) for i in range(xgv.shape[0])]
+    pairs += [(kvb, kv_h), (nwv, nw_h), (first_new, nf_h), (second_new, ns_h)]
+    copies = [pltpu.make_async_copy(a, b, sem.at[i]) for i, (a, b) in enumerate(pairs)]
+    for copy in copies:
+        copy.start()
+    for copy in copies:
         copy.wait()
 
 
@@ -324,28 +318,25 @@
     n_rep = partner.shape[0]
     dma = pltpu.SemaphoreType.DMA
     hops = NZ // 2
-    hbm = pl.BlockSpec(memory_space=pl.ANY)
-    smem = pl.BlockSpec(memory_space=pltpu.SMEM)
+    hbm = pl.BlockSpec(memory_space=pltpu.HBM)
+    vmem = pl.BlockSpec(memory_space=pltpu.VMEM)
     outs = pl.pallas_call(
         kernel,
         out_shape=(
-            jax.ShapeDtypeStruct((tok, cols), BF),
-            jax.ShapeDtypeStruct((tok, width), BF),
-            jax.ShapeDtypeStruct((rows, cols), BF),
-            jax.ShapeDtypeStruct((rows, cols), F32),
-            jax.ShapeDtypeStruct((rows, cols), F32),
+            pltpu.VMEM((tok, cols), BF),
+            pltpu.VMEM((width // rows, tok, rows), BF),
+            pltpu.VMEM((rows, cols), BF),
+            pltpu.VMEM((rows, cols), F32),
+            pltpu.VMEM((rows, cols), F32),
         ),
-        in_specs=[hbm] * 5 + [smem] * 2,
-        out_specs=[hbm] * 5,
+        in_specs=[hbm] * 7,
+        out_specs=[vmem] * 5,
         scratch_shapes=[
             pltpu.VMEM((NZ, 2 * tok, rows), BF),
             pltpu.VMEM((NZ, tok, rows), BF),
             pltpu.VMEM((2 * tok, cols), BF),
             pltpu.VMEM((2, NZ, rows, cols), BF),
             pltpu.VMEM((tok, cols), F32),
-            pltpu.VMEM((tok, cols), BF),
-            pltpu.VMEM((2, NZ, tok, rows), BF),
-            pltpu.VMEM((2, rows, cols), F32),
             pltpu.VMEM((2, rows, cols), F32),
             pltpu.VMEM((2, hops, rows, cols), BF),
             pltpu.VMEM((2, hops, rows, cols), BF),
@@ -354,8 +345,8 @@
             pltpu.VMEM((n_rep, rows // n_rep, cols), BF),
             pltpu.VMEM((n_rep, rows // n_rep, cols), BF),
             pltpu.VMEM((n_rep, rows // n_rep, cols), BF),
-            pltpu.VMEM((rows, cols), BF),
-            dma((4,)),
+            pltpu.SMEM((2, n_rep), jnp.int32),
+            dma((6,)),
             dma((2, NZ)),
             dma((NZ + 1,)),
             dma((NZ + 1,)),
@@ -367,14 +358,32 @@
             dma((2, hops, 2)),
             dma((2, n_rep)),
             dma((2, n_rep)),
-            dma((4,)),
-            dma((2, NZ)),
         ],
         name="step",
         compiler_params=pltpu.CompilerParams(
-            collective_id=0, has_side_effects=True, vmem_limit_bytes=52 << 20
+            collective_id=0, has_side_effects=True, vmem_limit_bytes=44 << 20
         ),
-    )(act, weights, cot, first_moment[0], second_moment[0], partner, mix_numerator)
+    )(
+        *(
+            pltpu.with_memory_space_constraint(x, pltpu.HBM)
+            for x in (act, weights, cot, first_moment[0], second_moment[0], partner, mix_numerator)
+        )
+    )
+    outs = pl.pallas_call(
+        write_out,
+        out_shape=(
+            jax.ShapeDtypeStruct((tok, cols), BF),
+            jax.ShapeDtypeStruct((tok, width), BF),
+            jax.ShapeDtypeStruct((rows, cols), BF),
+            jax.ShapeDtypeStruct((rows, cols), F32),
+            jax.ShapeDtypeStruct((rows, cols), F32),
+        ),
+        in_specs=[vmem] * 5,
+        out_specs=[hbm] * 5,
+        scratch_shapes=[dma((width // rows + 4,))],
+        name="write_out",
+        compiler_params=pltpu.CompilerParams(vmem_limit_bytes=1 << 20),
+    )(*outs)
     return tuple(out[None] for out in outs)
 
 

time: 137 us -> 128 us (0.934)
  local copies, waits for them, and re-layouts: 9.96 us -> 0 us
    unnamed x15 -> x0, local copies, waits for them, and re-layouts: 9.96 us -> none
    pallas_call x1 -> x2, Pallas kernels: 124 us -> 125 us  [the longest x1 122 us: per_device(): pl.pallas_call(kernel, out_shape=(pltpu.VMEM((tok, cols), BF), pltpu.VMEM...]
where the time goes in v2:
time: 128 us; the launch traced here: 126 us
  Pallas kernels  125 us (98%)
    pallas_call x1, Pallas kernels, per_device(): pl.pallas_call(kernel, out_shape=(pltpu.VMEM((tok, cols), BF), pltpu.VMEM...  122 us
    pallas_call x1, Pallas kernels, per_device(): pl.pallas_call(write_out, out_shape=(jax.ShapeDtypeStruct((tok, cols), BF...  2.93 us

profile of v2, /device:TPU:1, one launch (start us, length us, event | category | flops | bytes accessed | tf_op | source)
XLA Modules:
  0.0 125.7 jit_solution(7700154602948082239)
XLA Ops:
  0.6 122.2 %step.1 = (bf16[384,1024]{1,0:T(8,128)(2,1)S(1)}, bf16[16,384,256]{2,1,0:T(8,128)(2,1)S(1)}, bf16[256,1024]{1,0:T(8,128)(2,1)S(1)}, f32[256,1024]{1,0:T(8,128)S(1)}, f32[256,1024]{1,0:T(8,128)S(1)}) custom-call(bf16[384,4096]{1,0:T(8,128)(2,1)} %bitcast.10, bf16[256,1024]{1,0:T(8,128)(2,1)} %bitcast.14, bf16[384,1024]{1,0:T(8,128)(2,1)} %bitcast.13, ...), custom_call_target="tpu_custom_call" | custom-call | tf_op jit(solution)/shard_map/step/pallas_call | solution.py:323
  122.8 2.9 %write_out.1 = (bf16[384,1024]{1,0:T(8,128)(2,1)}, bf16[384,4096]{1,0:T(8,128)(2,1)}, bf16[256,1024]{1,0:T(8,128)(2,1)}, f32[256,1024]{1,0:T(8,128)}, f32[256,1024]{1,0:T(8,128)}) custom-call(bf16[384,1024]{1,0:T(8,128)(2,1)S(1)} %get-tuple-element.15.kvb, bf16[16,384,256]{2,1,0:T(8,128)(2,1)S(1)} %get-tuple-element.16.xgv, ...), custom_call_target="tpu_custom_call" | custom-call | tf_op jit(solution)/shard_map/write_out/pallas_call | solution.py:372

commit v3 on v0

v3 whole, which is shorter than its diff:
```python
import jax
import jax.numpy as jnp
from jax import lax
from jax.experimental import pallas as pl
from jax.experimental.pallas import tpu as pltpu
from jax.sharding import PartitionSpec as P

beta_one = 0.9
beta_two = 0.999
learn_rate = 0.02
weight_decay = 0.1
adam_eps = 1e-08
corr_one = 1.0 - beta_one**10
corr_two = 1.0 - beta_two**10
mix_denom = 64.0

MESH = pl.DeviceIdType.MESH
BF = jnp.bfloat16
F32 = jnp.float32
NZ = 8
HOPS = NZ // 2
ROWS_X = 96

SCHEDULE = (
    ("xs", 4), ("ag", 0, 0, 1), ("ag", 0, 1, 1), ("xs", "cot"), ("ag", 0, 0, 2), ("ag", 0, 1, 2),
    ("xs", 5), ("xs", 3), ("xs", 6), ("g", 4), ("rs", 1, 0, 1), ("rs", 0, 0, 0), ("g", 5),
    ("rs", 1, 1, 0), ("ag", 0, 0, 3), ("ag", 0, 1, 3), ("xs", 7), ("use", 0, 6), ("g", 6),
    ("xs", 2), ("use", 0, 1), ("wxB",), ("g", 3), ("rs", 0, 1, 0), ("rs", 0, 1, 1),
    ("rs", 1, 1, 1), ("xs", 1), ("use", 0, 7), ("ag", 1, 0, 1), ("wxA",), ("g", 2),
    ("ag", 1, 1, 1), ("g", 1), ("rs", 1, 2, 0), ("rs", 1, 2, 1), ("rs", 0, 2, 0), ("xs", 0),
    ("use", 1, 0), ("wx", 6), ("wx", 2), ("rs", 0, 2, 1), ("g", 7), ("rs", 0, 3, 0), ("wx", 7),
    ("rs", 1, 3, 0), ("rs", 1, 3, 1), ("ag", 1, 0, 2), ("g", 0), ("ag", 1, 1, 2), ("wx", 1),
    ("wx", 5), ("use", 1, 7), ("fin", 0), ("rs", 0, 3, 1), ("use", 0, 2), ("ex0", 0), ("wx", 3),
    ("ag", 0, 1, 4), ("ag", 0, 0, 4), ("ag", 1, 0, 3), ("use", 0, 5), ("ex1", 0), ("fin", 1),
    ("ex0", 1), ("ag", 1, 1, 3), ("use", 1, 1), ("use", 0, 0), ("use", 1, 2), ("ex1", 1),
    ("wx", 4), ("use", 0, 3), ("ag", 1, 0, 4), ("ag", 1, 1, 4), ("use", 1, 6), ("use", 0, 4),
)


def column_index(col, slot):
    me = lax.axis_index("fsdp")
    x = me % 2
    return lax.rem(me // 2 + slot, NZ) * 2 + (x if col == 0 else 1 - x)


def columns_of(ref, col, slot, rows):
    start = column_index(col, slot) * rows
    return ref.at[:, pl.ds(pl.multiple_of(start, rows), rows)]


def back_product(cot, block):
    return lax.dot_general(
        cot, block, (((1,), (1,)), ((), ())), preferred_element_type=F32
    ).astype(BF)


def kernel(
    act_h, w_h, cot_h, first_h, second_h, partner_h,
    kvacc, xgv, first_new, second_new, stepped, final, wg, aoth, ccat,
    acat, mom, rs_in, rs_out, gbuf, inbox_a, inbox_b, outbox, partner_s,
    load_sem, act_sem, x_send, x_recv, wx_send, wx_recv, ag_send, ag_recv,
    rs_send, rs_recv, ex_send, ex_recv,
):
    rep = lax.axis_index("rep")
    me = lax.axis_index("fsdp")
    inbox = (inbox_a, inbox_b)
    n_rep = inbox_a.shape[0]
    tok = cot_h.shape[0]
    rows, cols = w_h.shape
    half = cols // 2
    z, xl = me // 2, me % 2
    up = (rep, lax.rem(z + 1, NZ) * 2 + xl)
    down = (rep, lax.rem(z + NZ - 1, NZ) * 2 + xl)
    side = (rep, z * 2 + 1 - xl)
    ring = (up, down)

    def remote(src, dst, send, recv, target):
        return pltpu.make_async_remote_copy(
            src_ref=src, dst_ref=dst, send_sem=send, recv_sem=recv,
            device_id=target, device_id_type=MESH,
        )

    loads = {
        "cot": pltpu.make_async_copy(cot_h, ccat.at[pl.ds(0, tok)], load_sem.at[0]),
        "w": pltpu.make_async_copy(w_h, wg.at[0, 0], load_sem.at[1]),
        "first": pltpu.make_async_copy(first_h, mom.at[0], load_sem.at[2]),
        "second": pltpu.make_async_copy(second_h, mom.at[1], load_sem.at[3]),
        "partner": pltpu.make_async_copy(partner_h, partner_s, load_sem.at[4]),
    }
    for slot in range(NZ):
        loads[0, slot] = pltpu.make_async_copy(
            columns_of(act_h, 0, slot, rows), acat.at[slot, pl.ds(0, tok)], act_sem.at[0, slot]
        )
        loads[1, slot] = pltpu.make_async_copy(
            columns_of(act_h, 1, slot, rows), aoth.at[slot], act_sem.at[1, slot]
        )
    waited = set()

    def loaded(key):
        if key not in waited:
            waited.add(key)
            loads[key].wait()

    copies = {
        ("xs", "cot"): remote(
            cot_h, ccat.at[pl.ds(tok, tok)], x_send.at[NZ], x_recv.at[NZ], side
        ),
        ("wxA",): remote(
            w_h.at[pl.ds(0, ROWS_X)], wg.at[1, 0, pl.ds(0, ROWS_X)],
            wx_send.at[0], wx_recv.at[0], side,
        ),
        ("wxB",): remote(
            w_h.at[pl.ds(ROWS_X, rows - ROWS_X)], wg.at[1, 0, pl.ds(ROWS_X, rows - ROWS_X)],
            wx_send.at[NZ], wx_recv.at[NZ], side,
        ),
    }
    for slot in range(NZ):
        copies["xs", slot] = remote(
            columns_of(act_h, 1, slot, rows), acat.at[slot, pl.ds(tok, tok)],
            x_send.at[slot], x_recv.at[slot], side,
        )
        if slot > 0:
            copies["wx", slot] = remote(
                wg.at[0, slot, pl.ds(0, ROWS_X)], wg.at[1, slot, pl.ds(0, ROWS_X)],
                wx_send.at[slot], wx_recv.at[slot], side,
            )

    def gather(col, direction, hop):
        low, high = (0, rows) if col == 0 else (ROWS_X, rows)
        if hop == HOPS:
            middle = (low + high) // 2
            low, high = (low, middle) if direction == 0 else (middle, high)
        if direction == 0:
            src, dst = (NZ - hop + 1) % NZ, NZ - hop
        else:
            src, dst = hop - 1, hop
        span = pl.ds(low, high - low)
        source = w_h.at[span] if (col == 0 and hop == 1) else wg.at[col, src, span]
        return remote(
            source, wg.at[col, dst, span],
            ag_send.at[col, direction, hop - 1], ag_recv.at[col, direction, hop - 1],
            ring[direction],
        )

    def reduce_copy(direction, step, part):
        span = (direction, step, slice(None), pl.ds(part * half, half))
        return remote(
            rs_out.at[span], rs_in.at[span],
            rs_send.at[direction, step, part], rs_recv.at[direction, step, part],
            ring[direction],
        )

    for direction in range(2):
        for hop in range(1, HOPS + 1):
            for col in range(2):
                copies["ag", col, direction, hop] = gather(col, direction, hop)
        for step in range(HOPS):
            for part in range(2):
                if step > 0 or part == direction:
                    copies["rs", direction, step, part] = reduce_copy(direction, step, part)

    def exchange(phase, part):
        out = []
        for k in range(1, n_rep):
            peer = lax.rem(rep + k, n_rep)
            src = (stepped, outbox)[phase].at[part, peer]
            dst = final.at[part, rep] if phase else inbox[part].at[rep]
            out.append(
                remote(
                    src, dst,
                    ex_send.at[phase, part, k], ex_recv.at[phase, part, k], (peer, me),
                )
            )
        return out

    ex = {(phase, part): exchange(phase, part) for phase in range(2) for part in range(2)}

    def arrived(key):
        if key not in waited:
            waited.add(key)
            copies[key].wait_recv()

    def block_arrived(col, slot):
        if slot == 0:
            if col == 1:
                arrived(("wxB",))
        elif slot == HOPS:
            arrived(("ag", col, 0, HOPS))
            arrived(("ag", col, 1, HOPS))
        elif slot > HOPS:
            arrived(("ag", col, 0, NZ - slot))
        else:
            arrived(("ag", col, 1, slot))

    used = []

    def use_block(col, slot):
        block_arrived(col, slot)
        if col == 1:
            arrived(("wx", slot) if slot else ("wxA",))
        elif slot == 0:
            loaded("w")
        loaded("cot")
        loaded((col, slot))
        block = wg[col, slot]
        tokens = acat[slot, pl.ds(0, tok)] if col == 0 else aoth[slot]
        term = jnp.dot(tokens, block, preferred_element_type=F32)
        if used:
            kvacc[...] += term
        else:
            kvacc[...] = term
        used.append((col, slot))
        xgv[col, slot] = back_product(ccat[pl.ds(0, tok)], block)

    def product(slot):
        arrived(("xs", "cot"))
        arrived(("xs", slot))
        loaded("cot")
        loaded((0, slot))
        gbuf[slot] = lax.dot_general(
            acat[slot], ccat[...], (((0,), (0,)), ((), ())), preferred_element_type=F32
        )

    def reduce_send(direction, step, part):
        span = pl.ds(part * half, half)
        slot = HOPS - step if direction == 0 else HOPS + step
        value = gbuf[slot, :, span]
        if ("rs", direction, step - 1, part) in copies:
            arrived(("rs", direction, step - 1, part))
            value = value + rs_in[direction, step - 1, :, span].astype(F32)
        rs_out[direction, step, :, span] = value.astype(BF)
        copies["rs", direction, step, part].start()

    def finish(part):
        span = pl.ds(part * half, half)
        for name in ("first", "second", "w"):
            loaded(name)
        grad = gbuf[0, :, span]
        for direction in range(2):
            arrived(("rs", direction, HOPS - 1, part))
            grad = grad + rs_in[direction, HOPS - 1, :, span].astype(F32)
        new_a = beta_one * mom[0, :, span] + (1.0 - beta_one) * grad
        new_b = beta_two * mom[1, :, span] + (1.0 - beta_two) * grad * grad
        first_new[:, span] = new_a
        second_new[:, span] = new_b
        old = wg[0, 0, :, span].astype(F32)
        update = new_a / corr_one / (jnp.sqrt(new_b / corr_two) + adam_eps) + weight_decay * old
        stepped[part] = (old - learn_rate * update).astype(BF).reshape(stepped.shape[1:])

    def exchange_first(part):
        for copy in ex[0, part]:
            copy.start()
        inbox[part][rep] = stepped[part, rep]

    def exchange_second(part):
        loaded("partner")
        for copy in ex[0, part]:
            copy.wait_recv()
        for j in range(n_rep):
            outbox[part, j] = inbox[part][partner_s[j]]
        for copy in ex[1, part]:
            copy.start()
        final[part, rep] = outbox[part, rep]

    barrier = pltpu.get_barrier_semaphore()
    others = [(lax.rem(rep + k, n_rep), me) for k in range(1, n_rep)]
    for device in (up, down, side, *others):
        pl.semaphore_signal(barrier, inc=1, device_id=device, device_id_type=MESH)
    loads["cot"].start()
    loads["w"].start()
    for slot in (0, 7, 1, 4, 3, 5, 2, 6):
        loads[0, slot].start()
    pl.semaphore_wait(barrier, 3 + n_rep - 1)

    actions = {
        "use": use_block, "g": product, "rs": reduce_send, "fin": finish,
        "ex0": exchange_first, "ex1": exchange_second,
    }
    for position, token in enumerate(SCHEDULE):
        if position == LATE_LOADS:
            for slot in range(NZ):
                loads[1, slot].start()
            for name in ("first", "second", "partner"):
                loads[name].start()
        name = token[0]
        if name in actions:
            actions[name](*token[1:])
            continue
        if name == "ag":
            _, col, direction, hop = token
            if hop > 1:
                arrived(("ag", col, direction, hop - 1))
            elif col == 1:
                arrived(("wxB",))
        elif name == "wx":
            block_arrived(0, token[1])
        copies[token].start()

    for key, copy in copies.items():
        arrived(key)
        copy.wait_send()
    for part in range(2):
        for copy in ex[1, part]:
            copy.wait_recv()
        for phase in range(2):
            for copy in ex[phase, part]:
                copy.wait_send()
    for key in loads:
        loaded(key)


LATE_LOADS = 12
LEFT = tuple(
    (col, slot)
    for slot in (0, 7, 1, 6, 2, 5, 3, 4)
    for col in range(2)
    if ("use", col, slot) not in SCHEDULE
)


def write_out(
    kvacc, xgv, first_new, second_new, stepped, final, wg, aoth, ccat, mix_h,
    kv_h, xg_h, nw_h, nf_h, ns_h,
    kvb, xgl, nwv, mix_s, xg_sem, sem,
):
    tok = kvb.shape[0]
    rows, cols = nwv.shape
    half = cols // 2
    mix_load = pltpu.make_async_copy(mix_h, mix_s, sem.at[4])
    mix_load.start()
    copies = [
        pltpu.make_async_copy(first_new, nf_h, sem.at[0]),
        pltpu.make_async_copy(second_new, ns_h, sem.at[1]),
    ]
    for col in range(2):
        for slot in range(NZ):
            if (col, slot) not in LEFT:
                copies.append(
                    pltpu.make_async_copy(
                        xgv.at[col, slot], columns_of(xg_h, col, slot, rows), xg_sem.at[col, slot]
                    )
                )
    for copy in copies:
        copy.start()
    total = kvacc[...]
    for i, (col, slot) in enumerate(LEFT):
        block = wg[col, slot]
        total = total + jnp.dot(aoth[slot], block, preferred_element_type=F32)
        xgl[i] = back_product(ccat[pl.ds(0, tok)], block)
        copy = pltpu.make_async_copy(
            xgl.at[i], columns_of(xg_h, col, slot, rows), xg_sem.at[col, slot]
        )
        copy.start()
        copies.append(copy)
    kvb[...] = total.astype(BF)
    copies.append(pltpu.make_async_copy(kvb, kv_h, sem.at[2]))
    copies[-1].start()
    mix_load.wait()
    mixing = mix_s[lax.axis_index("rep")].astype(F32) / mix_denom
    for part in range(2):
        nwv[:, pl.ds(part * half, half)] = (
            ((1.0 - mixing) * stepped[part].astype(F32) + mixing * final[part].astype(F32))
            .astype(BF)
            .reshape(rows, half)
        )
    copies.append(pltpu.make_async_copy(nwv, nw_h, sem.at[3]))
    copies[-1].start()
    for copy in copies:
        copy.wait()


def per_device(
    activations, kv_weight, kv_cotangent, first_moment, second_moment, partner, mix_numerator
):
    act, weights, cot = activations[0], kv_weight[0], kv_cotangent[0]
    tok, width = act.shape
    rows, cols = weights.shape
    n_rep = partner.shape[0]
    chunks = (2, n_rep, rows // n_rep, cols // 2)
    dma = pltpu.SemaphoreType.DMA
    hbm = pl.BlockSpec(memory_space=pltpu.HBM)
    vmem = pl.BlockSpec(memory_space=pltpu.VMEM)

    def in_hbm(x):
        return pltpu.with_memory_space_constraint(x, pltpu.HBM)

    held = pl.pallas_call(
        kernel,
        out_shape=(
            pltpu.VMEM((tok, cols), F32),
            pltpu.VMEM((2, NZ, tok, rows), BF),
            pltpu.VMEM((rows, cols), F32),
            pltpu.VMEM((rows, cols), F32),
            pltpu.VMEM(chunks, BF),
            pltpu.VMEM(chunks, BF),
            pltpu.VMEM((2, NZ, rows, cols), BF),
            pltpu.VMEM((NZ, tok, rows), BF),
            pltpu.VMEM((2 * tok, cols), BF),
        ),
        in_specs=[hbm] * 6,
        out_specs=[vmem] * 9,
        scratch_shapes=[
            pltpu.VMEM((NZ, 2 * tok, rows), BF),
            pltpu.VMEM((2, rows, cols), F32),
            pltpu.VMEM((2, HOPS, rows, cols), BF),
            pltpu.VMEM((2, HOPS, rows, cols), BF),
            pltpu.VMEM((NZ, rows, cols), F32),
            pltpu.VMEM(chunks[1:], BF),
            pltpu.VMEM(chunks[1:], BF),
            pltpu.VMEM(chunks, BF),
            pltpu.SMEM((n_rep,), jnp.int32),
            dma((5,)),
            dma((2, NZ)),
            dma((NZ + 1,)),
            dma((NZ + 1,)),
            dma((NZ + 1,)),
            dma((NZ + 1,)),
            dma((2, 2, HOPS)),
            dma((2, 2, HOPS)),
            dma((2, HOPS, 2)),
            dma((2, HOPS, 2)),
            dma((2, 2, n_rep)),
            dma((2, 2, n_rep)),
        ],
        name="step",
        compiler_params=pltpu.CompilerParams(
            collective_id=0, has_side_effects=True, vmem_limit_bytes=32 << 20
        ),
    )(*(in_hbm(x) for x in (act, weights, cot, first_moment[0], second_moment[0], partner)))
    outs = pl.pallas_call(
        write_out,
        out_shape=(
            jax.ShapeDtypeStruct((tok, cols), BF),
            jax.ShapeDtypeStruct((tok, width), BF),
            jax.ShapeDtypeStruct((rows, cols), BF),
            jax.ShapeDtypeStruct((rows, cols), F32),
            jax.ShapeDtypeStruct((rows, cols), F32),
        ),
        in_specs=[vmem] * 9 + [hbm],
        out_specs=[hbm] * 5,
        scratch_shapes=[
            pltpu.VMEM((tok, cols), BF),
            pltpu.VMEM((len(LEFT), tok, rows), BF),
            pltpu.VMEM((rows, cols), BF),
            pltpu.SMEM((n_rep,), jnp.int32),
            dma((2, NZ)),
            dma((5,)),
        ],
        name="write_out",
        compiler_params=pltpu.CompilerParams(vmem_limit_bytes=8 << 20),
    )(*held, in_hbm(mix_numerator))
    return tuple(out[None] for out in outs)


def solution(mesh):
    split = P("rep", "fsdp", None)
    return jax.shard_map(
        per_device,
        mesh=mesh,
        in_specs=(split,) * 5 + (P(), P()),
        out_specs=(split,) * 5,
        check_vma=False,
    )
```

time: 485 us -> 125 us (0.26)
  waiting for transfers between devices: 435 us -> 0 us
  Pallas kernels: 0 us -> 124 us
  matrix products: 21.1 us -> 0 us
  between operations: 14.4 us -> 0.64 us
  other arithmetic: 11.5 us -> 0 us
    all_gather x2 -> x0, waiting for transfers between devices: 248 us -> none  [the longest x1 178 us: per_device(): piece = lax.all_gather(weights, 'fsdp', axis=0, tiled=True)]
    reduce_scatter x1 -> x0, waiting for transfers between devices: 186 us -> none  [per_device(): lax.psum_scatter(jnp.einsum('td,tc->dc', block, cotangent, preferred_elem...]
    pallas_call x0 -> x2, Pallas kernels: none -> 124 us  [the longest x1 120 us: per_device(): pl.pallas_call(kernel, out_shape=(pltpu.VMEM((tok, cols), F32), pltpu.VME...]
    dot_general x3 -> x0, matrix products: 21.1 us -> none  [the longest x1 8.88 us: per_device(): jnp.einsum('tc,rc->tr', cotangent, piece, preferred_element_type=jnp.floa...]
    reduce_sum x1 -> x0, other arithmetic: 5.62 us -> none  [per_device(): jnp.sum(jnp.where(matching[:, None, None], piece, jnp.zeros_like(piece)),...]
    broadcast_in_dim x2 -> x0, other arithmetic: 5.21 us -> none  [the longest x1 4.21 us: per_device(): moment_new_b[None]]
  transfers between devices with their start and end apart: 3 -> 0, of which waited for: 3 -> 0; matrix products, arithmetic and copies ran while one was open for 4% -> 0% of each run, Pallas kernels for 0% -> 0%
where the time goes in v3:
time: 125 us
  Pallas kernels  124 us (99%)
    pallas_call x1, Pallas kernels, per_device(): pl.pallas_call(kernel, out_shape=(pltpu.VMEM((tok, cols), F32), pltpu.VME...  120 us
    pallas_call x1, Pallas kernels, per_device(): pl.pallas_call(write_out, out_shape=(jax.ShapeDtypeStruct((tok, cols), BF...  3.53 us

profile of v3, /device:TPU:1, one launch (start us, length us, event | category | flops | bytes accessed | tf_op | source)
XLA Modules:
  0.0 124.6 jit_solution(15619476335922411528)
XLA Ops:
  0.6 120.5 %step.1 = (f32[384,1024]{1,0:T(8,128)S(1)}, bf16[2,8,384,256]{3,2,1,0:T(8,128)(2,1)S(1)}, f32[256,1024]{1,0:T(8,128)S(1)}, f32[256,1024]{1,0:T(8,128)S(1)}, bf16...) custom-call(bf16[384,4096]{1,0:T(8,128)(2,1)} %bitcast.10, ...), custom_call_target="tpu_custom_call" | custom-call | tf_op jit(solution)/shard_map/step/pallas_call | solution.py:387
  121.1 3.5 %write_out.1 = (bf16[384,1024]{1,0:T(8,128)(2,1)}, bf16[384,4096]{1,0:T(8,128)(2,1)}, bf16[256,1024]{1,0:T(8,128)(2,1)}, f32[256,1024]{1,0:T(8,128)}, f32[256,1024]{1,0:T(8,128)}) custom-call(f32[384,1024]{1,0:T(8,128)S(1)} %get-tuple-element.19.kvacc, bf16[2,8,384,256]{3,2,1,0:T(8,128)(2,1)S(1)} %get-tuple-element.20.xgv, ...), custom_call_target="tpu_custom_call" | custom-call | tf_op jit(solution)/shard_map/write_out/pallas_call | solution.py:430

commit v4 on v3

--- a/solution.py
+++ b/solution.py
@@ -22,18 +22,23 @@
 ROWS_X = 96
 
 SCHEDULE = (
-    ("xs", 4), ("ag", 0, 0, 1), ("ag", 0, 1, 1), ("xs", "cot"), ("ag", 0, 0, 2), ("ag", 0, 1, 2),
-    ("xs", 5), ("xs", 3), ("xs", 6), ("g", 4), ("rs", 1, 0, 1), ("rs", 0, 0, 0), ("g", 5),
-    ("rs", 1, 1, 0), ("ag", 0, 0, 3), ("ag", 0, 1, 3), ("xs", 7), ("use", 0, 6), ("g", 6),
-    ("xs", 2), ("use", 0, 1), ("wxB",), ("g", 3), ("rs", 0, 1, 0), ("rs", 0, 1, 1),
-    ("rs", 1, 1, 1), ("xs", 1), ("use", 0, 7), ("ag", 1, 0, 1), ("wxA",), ("g", 2),
-    ("ag", 1, 1, 1), ("g", 1), ("rs", 1, 2, 0), ("rs", 1, 2, 1), ("rs", 0, 2, 0), ("xs", 0),
-    ("use", 1, 0), ("wx", 6), ("wx", 2), ("rs", 0, 2, 1), ("g", 7), ("rs", 0, 3, 0), ("wx", 7),
-    ("rs", 1, 3, 0), ("rs", 1, 3, 1), ("ag", 1, 0, 2), ("g", 0), ("ag", 1, 1, 2), ("wx", 1),
-    ("wx", 5), ("use", 1, 7), ("fin", 0), ("rs", 0, 3, 1), ("use", 0, 2), ("ex0", 0), ("wx", 3),
-    ("ag", 0, 1, 4), ("ag", 0, 0, 4), ("ag", 1, 0, 3), ("use", 0, 5), ("ex1", 0), ("fin", 1),
-    ("ex0", 1), ("ag", 1, 1, 3), ("use", 1, 1), ("use", 0, 0), ("use", 1, 2), ("ex1", 1),
-    ("wx", 4), ("use", 0, 3), ("ag", 1, 0, 4), ("ag", 1, 1, 4), ("use", 1, 6), ("use", 0, 4),
+    ("wxB",), ("ag", 0, 1, 1, 0), ("ag", 0, 0, 1, 0), ("ag", 0, 0, 1, 1), ("xs", 4),
+    ("ag", 0, 1, 1, 1), ("ag", 0, 1, 2, 0), ("xs", 3), ("ag", 1, 0, 1, 0), ("ag", 1, 1, 1, 0),
+    ("xs", "cot"), ("ag", 0, 1, 2, 1), ("ag", 1, 1, 1, 1), ("ag", 0, 0, 2, 0),
+    ("ag", 1, 0, 2, 0), ("wxA",), ("ag", 0, 0, 2, 1), ("ag", 0, 1, 3, 0), ("xs", 5), ("xs", 2),
+    ("ag", 0, 0, 3, 0), ("xs", 1), ("xs", 6), ("ag", 1, 1, 2, 1), ("g", 4), ("rs", 0, 0, 0),
+    ("rs", 1, 0, 1), ("ag", 1, 0, 1, 1), ("xs", 0), ("g", 3), ("g", 5), ("rs", 0, 1, 0),
+    ("xs", 7), ("rs", 1, 1, 0), ("rs", 0, 1, 1), ("g", 2), ("rs", 1, 1, 1), ("use", 0, 0),
+    ("rs", 0, 2, 0), ("g", 1), ("ag", 0, 1, 3, 1), ("g", 6), ("rs", 1, 2, 1), ("rs", 1, 2, 0),
+    ("rs", 0, 2, 1), ("use", 0, 2), ("g", 0), ("use", 0, 6), ("ag", 1, 0, 2, 1), ("wx", 7),
+    ("use", 1, 0), ("wx", 6), ("use", 1, 7), ("rs", 0, 3, 1), ("wx", 3), ("wx", 2), ("g", 7),
+    ("rs", 1, 3, 1), ("use", 1, 6), ("use", 0, 3), ("rs", 1, 3, 0), ("rs", 0, 3, 0),
+    ("ag", 0, 0, 4, 0), ("ag", 1, 1, 2, 0), ("wx", 5), ("wx", 1), ("ag", 1, 1, 3, 1),
+    ("ag", 0, 0, 3, 1), ("fin", 1), ("ag", 1, 0, 3, 0), ("ex0", 1), ("use", 0, 7), ("fin", 0),
+    ("ag", 0, 1, 4, 1), ("ex0", 0), ("ag", 1, 0, 3, 1), ("use", 0, 1), ("wx", 4),
+    ("ag", 1, 1, 4, 1), ("ex1", 1), ("ex1", 0), ("ag", 1, 0, 4, 0), ("use", 1, 1),
+    ("ag", 1, 1, 3, 0), ("use", 1, 2), ("use", 0, 5), ("use", 0, 4), ("use", 1, 5),
+    ("use", 1, 3),
 )
 
 
@@ -125,21 +130,18 @@
                 wx_send.at[slot], wx_recv.at[slot], side,
             )
 
-    def gather(col, direction, hop):
+    def gather(col, direction, hop, part):
         low, high = (0, rows) if col == 0 else (ROWS_X, rows)
-        if hop == HOPS:
-            middle = (low + high) // 2
-            low, high = (low, middle) if direction == 0 else (middle, high)
+        length = (high - low) // 2
+        span = pl.ds(low + part * length, length)
         if direction == 0:
             src, dst = (NZ - hop + 1) % NZ, NZ - hop
         else:
             src, dst = hop - 1, hop
-        span = pl.ds(low, high - low)
         source = w_h.at[span] if (col == 0 and hop == 1) else wg.at[col, src, span]
+        sems = (col, direction, hop - 1, part)
         return remote(
-            source, wg.at[col, dst, span],
-            ag_send.at[col, direction, hop - 1], ag_recv.at[col, direction, hop - 1],
-            ring[direction],
+            source, wg.at[col, dst, span], ag_send.at[sems], ag_recv.at[sems], ring[direction]
         )
 
     def reduce_copy(direction, step, part):
@@ -153,7 +155,10 @@
     for direction in range(2):
         for hop in range(1, HOPS + 1):
             for col in range(2):
-                copies["ag", col, direction, hop] = gather(col, direction, hop)
+                for part in range(2):
+                    if hop < HOPS or part == direction:
+                        token = ("ag", col, direction, hop, part)
+                        copies[token] = gather(*token[1:])
         for step in range(HOPS):
             for part in range(2):
                 if step > 0 or part == direction:
@@ -180,17 +185,17 @@
             waited.add(key)
             copies[key].wait_recv()
 
-    def block_arrived(col, slot):
-        if slot == 0:
-            if col == 1:
-                arrived(("wxB",))
-        elif slot == HOPS:
-            arrived(("ag", col, 0, HOPS))
-            arrived(("ag", col, 1, HOPS))
-        elif slot > HOPS:
-            arrived(("ag", col, 0, NZ - slot))
-        else:
-            arrived(("ag", col, 1, slot))
+    def block_arrived(col, slot, parts=(0, 1)):
+        for part in parts:
+            if slot == 0:
+                if col == 1:
+                    arrived(("wxB",))
+            elif slot == HOPS:
+                arrived(("ag", col, part, HOPS, part))
+            elif slot > HOPS:
+                arrived(("ag", col, 0, NZ - slot, part))
+            else:
+                arrived(("ag", col, 1, slot, part))
 
     used = []
 
@@ -287,13 +292,13 @@
             actions[name](*token[1:])
             continue
         if name == "ag":
-            _, col, direction, hop = token
+            _, col, direction, hop, part = token
             if hop > 1:
-                arrived(("ag", col, direction, hop - 1))
+                arrived(("ag", col, direction, hop - 1, part))
             elif col == 1:
                 arrived(("wxB",))
         elif name == "wx":
-            block_arrived(0, token[1])
+            block_arrived(0, token[1], (0,))
         copies[token].start()
 
     for key, copy in copies.items():
@@ -309,7 +314,7 @@
         loaded(key)
 
 
-LATE_LOADS = 12
+LATE_LOADS = 16
 LEFT = tuple(
     (col, slot)
     for slot in (0, 7, 1, 6, 2, 5, 3, 4)
@@ -415,8 +420,8 @@
             dma((NZ + 1,)),
             dma((NZ + 1,)),
             dma((NZ + 1,)),
-            dma((2, 2, HOPS)),
-            dma((2, 2, HOPS)),
+            dma((2, 2, HOPS, 2)),
+            dma((2, 2, HOPS, 2)),
             dma((2, HOPS, 2)),
             dma((2, HOPS, 2)),
             dma((2, 2, n_rep)),

time: 125 us -> 124 us (level)
  no operation moved by 1% of the time
where the time goes in v4:
time: 124 us
  Pallas kernels  123 us (99%)
    pallas_call x1, Pallas kernels, per_device(): pl.pallas_call(kernel, out_shape=(pltpu.VMEM((tok, cols), F32), pltpu.VME...  120 us
    pallas_call x1, Pallas kernels, per_device(): pl.pallas_call(write_out, out_shape=(jax.ShapeDtypeStruct((tok, cols), BF...  3.41 us

profile of v4, /device:TPU:1, one launch (start us, length us, event | category | flops | bytes accessed | tf_op | source)
XLA Modules:
  0.0 123.8 jit_solution(10041716942767731024)
XLA Ops:
  0.6 119.6 %step.1 = (f32[384,1024]{1,0:T(8,128)S(1)}, bf16[2,8,384,256]{3,2,1,0:T(8,128)(2,1)S(1)}, f32[256,1024]{1,0:T(8,128)S(1)}, f32[256,1024]{1,0:T(8,128)S(1)}, bf16...) custom-call(bf16[384,4096]{1,0:T(8,128)(2,1)} %bitcast.10, ...), custom_call_target="tpu_custom_call" | custom-call | tf_op jit(solution)/shard_map/step/pallas_call | solution.py:392
  120.3 3.4 %write_out.1 = (bf16[384,1024]{1,0:T(8,128)(2,1)}, bf16[384,4096]{1,0:T(8,128)(2,1)}, bf16[256,1024]{1,0:T(8,128)(2,1)}, f32[256,1024]{1,0:T(8,128)}, f32[256,1024]{1,0:T(8,128)}) custom-call(f32[384,1024]{1,0:T(8,128)S(1)} %get-tuple-element.19.kvacc, bf16[2,8,384,256]{3,2,1,0:T(8,128)(2,1)S(1)} %get-tuple-element.20.xgv, ...), custom_call_target="tpu_custom_call" | custom-call | tf_op jit(solution)/shard_map/write_out/pallas_call | solution.py:435

commit v5 on v4

--- a/solution.py
+++ b/solution.py
@@ -22,23 +22,22 @@
 ROWS_X = 96
 
 SCHEDULE = (
-    ("wxB",), ("ag", 0, 1, 1, 0), ("ag", 0, 0, 1, 0), ("ag", 0, 0, 1, 1), ("xs", 4),
-    ("ag", 0, 1, 1, 1), ("ag", 0, 1, 2, 0), ("xs", 3), ("ag", 1, 0, 1, 0), ("ag", 1, 1, 1, 0),
-    ("xs", "cot"), ("ag", 0, 1, 2, 1), ("ag", 1, 1, 1, 1), ("ag", 0, 0, 2, 0),
-    ("ag", 1, 0, 2, 0), ("wxA",), ("ag", 0, 0, 2, 1), ("ag", 0, 1, 3, 0), ("xs", 5), ("xs", 2),
-    ("ag", 0, 0, 3, 0), ("xs", 1), ("xs", 6), ("ag", 1, 1, 2, 1), ("g", 4), ("rs", 0, 0, 0),
-    ("rs", 1, 0, 1), ("ag", 1, 0, 1, 1), ("xs", 0), ("g", 3), ("g", 5), ("rs", 0, 1, 0),
-    ("xs", 7), ("rs", 1, 1, 0), ("rs", 0, 1, 1), ("g", 2), ("rs", 1, 1, 1), ("use", 0, 0),
-    ("rs", 0, 2, 0), ("g", 1), ("ag", 0, 1, 3, 1), ("g", 6), ("rs", 1, 2, 1), ("rs", 1, 2, 0),
-    ("rs", 0, 2, 1), ("use", 0, 2), ("g", 0), ("use", 0, 6), ("ag", 1, 0, 2, 1), ("wx", 7),
-    ("use", 1, 0), ("wx", 6), ("use", 1, 7), ("rs", 0, 3, 1), ("wx", 3), ("wx", 2), ("g", 7),
-    ("rs", 1, 3, 1), ("use", 1, 6), ("use", 0, 3), ("rs", 1, 3, 0), ("rs", 0, 3, 0),
-    ("ag", 0, 0, 4, 0), ("ag", 1, 1, 2, 0), ("wx", 5), ("wx", 1), ("ag", 1, 1, 3, 1),
-    ("ag", 0, 0, 3, 1), ("fin", 1), ("ag", 1, 0, 3, 0), ("ex0", 1), ("use", 0, 7), ("fin", 0),
-    ("ag", 0, 1, 4, 1), ("ex0", 0), ("ag", 1, 0, 3, 1), ("use", 0, 1), ("wx", 4),
-    ("ag", 1, 1, 4, 1), ("ex1", 1), ("ex1", 0), ("ag", 1, 0, 4, 0), ("use", 1, 1),
-    ("ag", 1, 1, 3, 0), ("use", 1, 2), ("use", 0, 5), ("use", 0, 4), ("use", 1, 5),
-    ("use", 1, 3),
+    ("wxB",), ("ag", 0, 0, 1, 0), ("ag", 0, 1, 1, 0), ("xs", "cot"), ("xs", 4), ("xs", 3),
+    ("ag", 0, 1, 1, 1), ("xs", 5), ("ag", 0, 0, 1, 1), ("xs", 2), ("ag", 0, 0, 2, 0), ("xs", 1),
+    ("ag", 0, 1, 2, 0), ("wxA",), ("ag", 1, 1, 1, 1), ("ag", 1, 0, 1, 0), ("ag", 0, 1, 2, 1),
+    ("ag", 0, 0, 2, 1), ("ag", 1, 0, 1, 1), ("ag", 0, 1, 3, 0), ("xs", 6), ("xs", 7),
+    ("ag", 1, 1, 1, 0), ("ag", 0, 0, 3, 0), ("g", 4), ("rs", 0, 0, 0), ("rs", 1, 0, 1), ("g", 3),
+    ("rs", 0, 1, 1), ("ag", 1, 1, 2, 1), ("g", 5), ("rs", 1, 1, 0), ("ag", 1, 0, 2, 0),
+    ("rs", 1, 1, 1), ("wx", 7), ("g", 2), ("ag", 0, 1, 3, 1), ("rs", 0, 1, 0), ("g", 1),
+    ("rs", 0, 2, 1), ("g", 6), ("rs", 1, 2, 1), ("rs", 0, 2, 0), ("xs", 0), ("g", 7),
+    ("ag", 0, 0, 3, 1), ("use", 0, 0), ("wx", 1), ("wx", 6), ("wx", 5), ("rs", 1, 2, 0),
+    ("use", 0, 2), ("use", 0, 6), ("rs", 0, 3, 1), ("rs", 1, 3, 1), ("rs", 0, 3, 0), ("g", 0),
+    ("rs", 1, 3, 0), ("ag", 1, 1, 2, 0), ("ag", 1, 1, 3, 1), ("ag", 0, 0, 4, 0), ("wx", 2),
+    ("ag", 1, 0, 2, 1), ("wx", 3), ("use", 0, 3), ("use", 0, 1), ("use", 1, 7), ("use", 0, 7),
+    ("ag", 1, 0, 3, 0), ("use", 1, 0), ("fin", 1), ("ex0", 1), ("use", 0, 5), ("ag", 0, 1, 4, 1),
+    ("fin", 0), ("ex0", 0), ("ag", 1, 1, 3, 0), ("wx", 4), ("use", 1, 1), ("ex1", 1),
+    ("ag", 1, 0, 3, 1), ("ex1", 0), ("ag", 1, 0, 4, 0), ("ag", 1, 1, 4, 1), ("use", 1, 6),
+    ("use", 1, 2), ("use", 0, 4), ("use", 1, 5), ("use", 1, 3),
 )
 
 

time: 124 us -> 124 us (level)
  no operation moved by 1% of the time
where the time goes in v5:
time: 124 us
  Pallas kernels  123 us (99%)
    pallas_call x1, Pallas kernels, per_device(): pl.pallas_call(kernel, out_shape=(pltpu.VMEM((tok, cols), F32), pltpu.VME...  120 us
    pallas_call x1, Pallas kernels, per_device(): pl.pallas_call(write_out, out_shape=(jax.ShapeDtypeStruct((tok, cols), BF...  3.41 us

profile of v5, /device:TPU:1, one launch (start us, length us, event | category | flops | bytes accessed | tf_op | source)
XLA Modules:
  0.0 123.7 jit_solution(1791723519680066609)
XLA Ops:
  0.6 119.6 %step.1 = (f32[384,1024]{1,0:T(8,128)S(1)}, bf16[2,8,384,256]{3,2,1,0:T(8,128)(2,1)S(1)}, f32[256,1024]{1,0:T(8,128)S(1)}, f32[256,1024]{1,0:T(8,128)S(1)}, bf16...) custom-call(bf16[384,4096]{1,0:T(8,128)(2,1)} %bitcast.10, ...), custom_call_target="tpu_custom_call" | custom-call | tf_op jit(solution)/shard_map/step/pallas_call | solution.py:391
  120.2 3.4 %write_out.1 = (bf16[384,1024]{1,0:T(8,128)(2,1)}, bf16[384,4096]{1,0:T(8,128)(2,1)}, bf16[256,1024]{1,0:T(8,128)(2,1)}, f32[256,1024]{1,0:T(8,128)}, f32[256,1024]{1,0:T(8,128)}) custom-call(f32[384,1024]{1,0:T(8,128)S(1)} %get-tuple-element.19.kvacc, bf16[2,8,384,256]{3,2,1,0:T(8,128)(2,1)S(1)} %get-tuple-element.20.xgv, ...), custom_call_target="tpu_custom_call" | custom-call | tf_op jit(solution)/shard_map/write_out/pallas_call | solution.py:434

commit v6 on v5

--- a/solution.py
+++ b/solution.py
@@ -19,25 +19,25 @@
 F32 = jnp.float32
 NZ = 8
 HOPS = NZ // 2
-ROWS_X = 96
 
 SCHEDULE = (
-    ("wxB",), ("ag", 0, 0, 1, 0), ("ag", 0, 1, 1, 0), ("xs", "cot"), ("xs", 4), ("xs", 3),
-    ("ag", 0, 1, 1, 1), ("xs", 5), ("ag", 0, 0, 1, 1), ("xs", 2), ("ag", 0, 0, 2, 0), ("xs", 1),
-    ("ag", 0, 1, 2, 0), ("wxA",), ("ag", 1, 1, 1, 1), ("ag", 1, 0, 1, 0), ("ag", 0, 1, 2, 1),
-    ("ag", 0, 0, 2, 1), ("ag", 1, 0, 1, 1), ("ag", 0, 1, 3, 0), ("xs", 6), ("xs", 7),
-    ("ag", 1, 1, 1, 0), ("ag", 0, 0, 3, 0), ("g", 4), ("rs", 0, 0, 0), ("rs", 1, 0, 1), ("g", 3),
-    ("rs", 0, 1, 1), ("ag", 1, 1, 2, 1), ("g", 5), ("rs", 1, 1, 0), ("ag", 1, 0, 2, 0),
-    ("rs", 1, 1, 1), ("wx", 7), ("g", 2), ("ag", 0, 1, 3, 1), ("rs", 0, 1, 0), ("g", 1),
-    ("rs", 0, 2, 1), ("g", 6), ("rs", 1, 2, 1), ("rs", 0, 2, 0), ("xs", 0), ("g", 7),
-    ("ag", 0, 0, 3, 1), ("use", 0, 0), ("wx", 1), ("wx", 6), ("wx", 5), ("rs", 1, 2, 0),
-    ("use", 0, 2), ("use", 0, 6), ("rs", 0, 3, 1), ("rs", 1, 3, 1), ("rs", 0, 3, 0), ("g", 0),
-    ("rs", 1, 3, 0), ("ag", 1, 1, 2, 0), ("ag", 1, 1, 3, 1), ("ag", 0, 0, 4, 0), ("wx", 2),
-    ("ag", 1, 0, 2, 1), ("wx", 3), ("use", 0, 3), ("use", 0, 1), ("use", 1, 7), ("use", 0, 7),
-    ("ag", 1, 0, 3, 0), ("use", 1, 0), ("fin", 1), ("ex0", 1), ("use", 0, 5), ("ag", 0, 1, 4, 1),
-    ("fin", 0), ("ex0", 0), ("ag", 1, 1, 3, 0), ("wx", 4), ("use", 1, 1), ("ex1", 1),
-    ("ag", 1, 0, 3, 1), ("ex1", 0), ("ag", 1, 0, 4, 0), ("ag", 1, 1, 4, 1), ("use", 1, 6),
-    ("use", 1, 2), ("use", 0, 4), ("use", 1, 5), ("use", 1, 3),
+    ("xs", "cot"), ("xs", 4), ("xs", 3), ("ag", 0, 1, 1, 0), ("ag", 0, 0, 1, 1),
+    ("ag", 0, 0, 1, 0), ("ag", 0, 1, 1, 1), ("xs", 5), ("ag", 0, 0, 2, 1), ("xs", 2), ("xs", 1),
+    ("xs", 6), ("xs", 0), ("ag", 0, 1, 2, 0), ("ag", 0, 1, 2, 1), ("ag", 0, 0, 2, 0),
+    ("ag", 0, 0, 3, 1), ("g", 4), ("rs", 1, 0, 1), ("ag", 0, 1, 3, 1), ("rs", 0, 0, 0), ("g", 5),
+    ("rs", 1, 1, 1), ("xs", 7), ("wxB",), ("g", 3), ("rs", 0, 1, 1), ("use", 0, 7),
+    ("rs", 1, 1, 0), ("rs", 0, 1, 0), ("use", 0, 0), ("g", 2), ("g", 1), ("g", 6),
+    ("rs", 0, 2, 1), ("rs", 1, 2, 1), ("px", 6), ("px", 5), ("rs", 1, 2, 0), ("rs", 0, 2, 0),
+    ("g", 7), ("g", 0), ("rs", 0, 3, 1), ("px", 2), ("rs", 1, 3, 1), ("use", 0, 6),
+    ("rs", 1, 3, 0), ("px", 0), ("rs", 0, 3, 0), ("ag", 1, 0, 1, 1), ("ag", 1, 0, 1, 0),
+    ("px", 7), ("px", 1), ("use", 1, 0), ("fin", 1), ("ex0", 1), ("ag", 0, 1, 4, 1),
+    ("ag", 0, 0, 3, 0), ("px", 3), ("ag", 1, 1, 1, 1), ("fin", 0), ("ex0", 0), ("use", 0, 2),
+    ("ag", 1, 0, 2, 1), ("ag", 1, 1, 1, 0), ("ag", 0, 1, 3, 0), ("ex1", 1), ("use", 1, 7),
+    ("ag", 1, 0, 2, 0), ("px", 4), ("pk", 0), ("ex1", 0), ("ag", 1, 1, 2, 1), ("pk", 1),
+    ("ag", 1, 0, 3, 1), ("ag", 1, 0, 3, 0), ("ag", 1, 1, 2, 0), ("ag", 0, 0, 4, 0),
+    ("use", 1, 6), ("ag", 1, 1, 3, 1), ("use", 0, 3), ("ag", 1, 1, 3, 0), ("use", 0, 5),
+    ("use", 1, 1), ("ag", 1, 0, 4, 0), ("use", 0, 1), ("ag", 1, 1, 4, 1), ("use", 1, 5),
+    ("use", 0, 4), ("use", 1, 3), ("use", 1, 2),
 )
 
 
@@ -47,8 +47,11 @@
     return lax.rem(me // 2 + slot, NZ) * 2 + (x if col == 0 else 1 - x)
 
 
-def columns_of(ref, col, slot, rows):
+def columns_of(ref, col, slot, rows, part=None):
     start = column_index(col, slot) * rows
+    if part is not None:
+        rows = rows // 2
+        start = start + part * rows
     return ref.at[:, pl.ds(pl.multiple_of(start, rows), rows)]
 
 
@@ -60,10 +63,10 @@
 
 def kernel(
     act_h, w_h, cot_h, first_h, second_h, partner_h,
-    kvacc, xgv, first_new, second_new, stepped, final, wg, aoth, ccat,
-    acat, mom, rs_in, rs_out, gbuf, inbox_a, inbox_b, outbox, partner_s,
+    kvacc, xga, xgb, xgc, kvc, first_new, second_new, stepped, final, wg, aoth, ccat,
+    px_out, pk_out, pk_acc, acat, mom, rs_in, rs_out, gbuf, inbox_a, inbox_b, outbox, partner_s,
     load_sem, act_sem, x_send, x_recv, wx_send, wx_recv, ag_send, ag_recv,
-    rs_send, rs_recv, ex_send, ex_recv,
+    rs_send, rs_recv, ex_send, ex_recv, px_send, px_recv, pk_send, pk_recv,
 ):
     rep = lax.axis_index("rep")
     me = lax.axis_index("fsdp")
@@ -72,6 +75,7 @@
     tok = cot_h.shape[0]
     rows, cols = w_h.shape
     half = cols // 2
+    low_rows, high_rows = pl.ds(0, rows // 2), pl.ds(rows // 2, rows // 2)
     z, xl = me // 2, me % 2
     up = (rep, lax.rem(z + 1, NZ) * 2 + xl)
     down = (rep, lax.rem(z + NZ - 1, NZ) * 2 + xl)
@@ -96,7 +100,7 @@
             columns_of(act_h, 0, slot, rows), acat.at[slot, pl.ds(0, tok)], act_sem.at[0, slot]
         )
         loads[1, slot] = pltpu.make_async_copy(
-            columns_of(act_h, 1, slot, rows), aoth.at[slot], act_sem.at[1, slot]
+            columns_of(act_h, 1, slot, rows, 0), aoth.at[slot], act_sem.at[1, slot]
         )
     waited = set()
 
@@ -109,13 +113,8 @@
         ("xs", "cot"): remote(
             cot_h, ccat.at[pl.ds(tok, tok)], x_send.at[NZ], x_recv.at[NZ], side
         ),
-        ("wxA",): remote(
-            w_h.at[pl.ds(0, ROWS_X)], wg.at[1, 0, pl.ds(0, ROWS_X)],
-            wx_send.at[0], wx_recv.at[0], side,
-        ),
         ("wxB",): remote(
-            w_h.at[pl.ds(ROWS_X, rows - ROWS_X)], wg.at[1, 0, pl.ds(ROWS_X, rows - ROWS_X)],
-            wx_send.at[NZ], wx_recv.at[NZ], side,
+            w_h.at[low_rows], wg.at[1, 0, low_rows], wx_send.at[0], wx_recv.at[0], side
         ),
     }
     for slot in range(NZ):
@@ -123,16 +122,18 @@
             columns_of(act_h, 1, slot, rows), acat.at[slot, pl.ds(tok, tok)],
             x_send.at[slot], x_recv.at[slot], side,
         )
-        if slot > 0:
-            copies["wx", slot] = remote(
-                wg.at[0, slot, pl.ds(0, ROWS_X)], wg.at[1, slot, pl.ds(0, ROWS_X)],
-                wx_send.at[slot], wx_recv.at[slot], side,
-            )
+        copies["px", slot] = remote(
+            px_out.at[slot], xgc.at[slot], px_send.at[slot], px_recv.at[slot], side
+        )
+    for part in range(2):
+        span = (slice(None), pl.ds(part * half, half))
+        copies["pk", part] = remote(
+            pk_out.at[span], kvc.at[span], pk_send.at[part], pk_recv.at[part], side
+        )
 
     def gather(col, direction, hop, part):
-        low, high = (0, rows) if col == 0 else (ROWS_X, rows)
-        length = (high - low) // 2
-        span = pl.ds(low + part * length, length)
+        length = rows // 2 if col == 0 else rows // 4
+        span = pl.ds(part * length, length)
         if direction == 0:
             src, dst = (NZ - hop + 1) % NZ, NZ - hop
         else:
@@ -200,21 +201,44 @@
 
     def use_block(col, slot):
         block_arrived(col, slot)
-        if col == 1:
-            arrived(("wx", slot) if slot else ("wxA",))
-        elif slot == 0:
+        if col == 0 and slot == 0:
             loaded("w")
         loaded("cot")
         loaded((col, slot))
-        block = wg[col, slot]
-        tokens = acat[slot, pl.ds(0, tok)] if col == 0 else aoth[slot]
+        if col == 0:
+            tokens, block = acat[slot, pl.ds(0, tok)], wg[0, slot]
+        else:
+            tokens, block = aoth[slot], wg[1, slot, low_rows]
         term = jnp.dot(tokens, block, preferred_element_type=F32)
         if used:
             kvacc[...] += term
         else:
             kvacc[...] = term
         used.append((col, slot))
-        xgv[col, slot] = back_product(ccat[pl.ds(0, tok)], block)
+        (xga, xgb)[col][slot] = back_product(ccat[pl.ds(0, tok)], block)
+
+    sided = []
+
+    def side_products(slot):
+        block_arrived(0, slot, (1,))
+        arrived(("xs", "cot"))
+        arrived(("xs", slot))
+        if slot == 0:
+            loaded("w")
+        block = wg[0, slot, high_rows]
+        px_out[slot] = back_product(ccat[pl.ds(tok, tok)], block)
+        copies["px", slot].start()
+        term = jnp.dot(acat[slot, pl.ds(tok, tok), high_rows], block, preferred_element_type=F32)
+        if sided:
+            pk_acc[...] += term
+        else:
+            pk_acc[...] = term
+        sided.append(slot)
+
+    def side_sum(part):
+        span = pl.ds(part * half, half)
+        pk_out[:, span] = pk_acc[:, span].astype(BF)
+        copies["pk", part].start()
 
     def product(slot):
         arrived(("xs", "cot"))
@@ -278,7 +302,7 @@
 
     actions = {
         "use": use_block, "g": product, "rs": reduce_send, "fin": finish,
-        "ex0": exchange_first, "ex1": exchange_second,
+        "ex0": exchange_first, "ex1": exchange_second, "px": side_products, "pk": side_sum,
     }
     for position, token in enumerate(SCHEDULE):
         if position == LATE_LOADS:
@@ -296,8 +320,6 @@
                 arrived(("ag", col, direction, hop - 1, part))
             elif col == 1:
                 arrived(("wxB",))
-        elif name == "wx":
-            block_arrived(0, token[1], (0,))
         copies[token].start()
 
     for key, copy in copies.items():
@@ -323,7 +345,7 @@
 
 
 def write_out(
-    kvacc, xgv, first_new, second_new, stepped, final, wg, aoth, ccat, mix_h,
+    kvacc, xga, xgb, xgc, kvc, first_new, second_new, stepped, final, wg, aoth, ccat, mix_h,
     kv_h, xg_h, nw_h, nf_h, ns_h,
     kvb, xgl, nwv, mix_s, xg_sem, sem,
 ):
@@ -336,23 +358,27 @@
         pltpu.make_async_copy(first_new, nf_h, sem.at[0]),
         pltpu.make_async_copy(second_new, ns_h, sem.at[1]),
     ]
-    for col in range(2):
-        for slot in range(NZ):
-            if (col, slot) not in LEFT:
-                copies.append(
-                    pltpu.make_async_copy(
-                        xgv.at[col, slot], columns_of(xg_h, col, slot, rows), xg_sem.at[col, slot]
-                    )
+    for slot in range(NZ):
+        blocks = [(xga, 0, None, 0), (xgc, 1, 1, 2)]
+        if (1, slot) not in LEFT:
+            blocks.append((xgb, 1, 0, 1))
+        for source, col, part, sem_row in blocks:
+            copies.append(
+                pltpu.make_async_copy(
+                    source.at[slot],
+                    columns_of(xg_h, col, slot, rows, part),
+                    xg_sem.at[sem_row, slot],
                 )
+            )
     for copy in copies:
         copy.start()
-    total = kvacc[...]
+    total = kvacc[...] + kvc[...].astype(F32)
     for i, (col, slot) in enumerate(LEFT):
-        block = wg[col, slot]
+        block = wg[col, slot, pl.ds(0, rows // 2)]
         total = total + jnp.dot(aoth[slot], block, preferred_element_type=F32)
         xgl[i] = back_product(ccat[pl.ds(0, tok)], block)
         copy = pltpu.make_async_copy(
-            xgl.at[i], columns_of(xg_h, col, slot, rows), xg_sem.at[col, slot]
+            xgl.at[i], columns_of(xg_h, col, slot, rows, 0), xg_sem.at[col, slot]
         )
         copy.start()
         copies.append(copy)
@@ -392,18 +418,24 @@
         kernel,
         out_shape=(
             pltpu.VMEM((tok, cols), F32),
-            pltpu.VMEM((2, NZ, tok, rows), BF),
+            pltpu.VMEM((NZ, tok, rows), BF),
+            pltpu.VMEM((NZ, tok, rows // 2), BF),
+            pltpu.VMEM((NZ, tok, rows // 2), BF),
+            pltpu.VMEM((tok, cols), BF),
             pltpu.VMEM((rows, cols), F32),
             pltpu.VMEM((rows, cols), F32),
             pltpu.VMEM(chunks, BF),
             pltpu.VMEM(chunks, BF),
             pltpu.VMEM((2, NZ, rows, cols), BF),
-            pltpu.VMEM((NZ, tok, rows), BF),
+            pltpu.VMEM((NZ, tok, rows // 2), BF),
             pltpu.VMEM((2 * tok, cols), BF),
         ),
         in_specs=[hbm] * 6,
-        out_specs=[vmem] * 9,
+        out_specs=[vmem] * 12,
         scratch_shapes=[
+            pltpu.VMEM((NZ, tok, rows // 2), BF),
+            pltpu.VMEM((tok, cols), BF),
+            pltpu.VMEM((tok, cols), F32),
             pltpu.VMEM((NZ, 2 * tok, rows), BF),
             pltpu.VMEM((2, rows, cols), F32),
             pltpu.VMEM((2, HOPS, rows, cols), BF),
@@ -417,14 +449,18 @@
             dma((2, NZ)),
             dma((NZ + 1,)),
             dma((NZ + 1,)),
-            dma((NZ + 1,)),
-            dma((NZ + 1,)),
+            dma((1,)),
+            dma((1,)),
             dma((2, 2, HOPS, 2)),
             dma((2, 2, HOPS, 2)),
             dma((2, HOPS, 2)),
             dma((2, HOPS, 2)),
             dma((2, 2, n_rep)),
             dma((2, 2, n_rep)),
+            dma((NZ,)),
+            dma((NZ,)),
+            dma((2,)),
+            dma((2,)),
         ],
         name="step",
         compiler_params=pltpu.CompilerParams(
@@ -440,14 +476,14 @@
             jax.ShapeDtypeStruct((rows, cols), F32),
             jax.ShapeDtypeStruct((rows, cols), F32),
         ),
-        in_specs=[vmem] * 9 + [hbm],
+        in_specs=[vmem] * 12 + [hbm],
         out_specs=[hbm] * 5,
         scratch_shapes=[
             pltpu.VMEM((tok, cols), BF),
-            pltpu.VMEM((len(LEFT), tok, rows), BF),
+            pltpu.VMEM((len(LEFT), tok, rows // 2), BF),
             pltpu.VMEM((rows, cols), BF),
             pltpu.SMEM((n_rep,), jnp.int32),
-            dma((2, NZ)),
+            dma((3, NZ)),
             dma((5,)),
         ],
         name="write_out",

time: 124 us -> 119 us (0.960)
  Pallas kernels: 123 us -> 118 us
    pallas_call x1, Pallas kernels: 120 us -> 115 us  [per_device(): pl.pallas_call(kernel, out_shape=(pltpu.VMEM((tok, cols), F32), pltpu.VME...]
where the time goes in v6:
time: 119 us
  Pallas kernels  118 us (99%)
    pallas_call x1, Pallas kernels, per_device(): pl.pallas_call(kernel, out_shape=(pltpu.VMEM((tok, cols), F32), pltpu.VME...  115 us
    pallas_call x1, Pallas kernels, per_device(): pl.pallas_call(write_out, out_shape=(jax.ShapeDtypeStruct((tok, cols), BF...  3.47 us

profile of v6, /device:TPU:1, one launch (start us, length us, event | category | flops | bytes accessed | tf_op | source)
XLA Modules:
  0.0 119.0 jit_solution(2196708525293285396)
XLA Ops:
  0.6 114.7 %step.1 = (f32[384,1024]{1,0:T(8,128)S(1)}, bf16[8,384,256]{2,1,0:T(8,128)(2,1)S(1)}, bf16[8,384,128]{2,1,0:T(8,128)(2,1)S(1)}, bf16[8,384,128]{2,1,0:T(8,128)(2...) custom-call(bf16[384,4096]{1,0:T(8,128)(2,1)} %bitcast.10, ...), custom_call_target="tpu_custom_call" | custom-call | tf_op jit(solution)/shard_map/step/pallas_call | solution.py:417
  115.3 3.5 %write_out.1 = (bf16[384,1024]{1,0:T(8,128)(2,1)}, bf16[384,4096]{1,0:T(8,128)(2,1)}, bf16[256,1024]{1,0:T(8,128)(2,1)}, f32[256,1024]{1,0:T(8,128)}, f32[256,1024]{1,0:T(8,128)}) custom-call(f32[384,1024]{1,0:T(8,128)S(1)} %get-tuple-element.22.kvacc, bf16[8,384,256]{2,1,0:T(8,128)(2,1)S(1)} %get-tuple-element.23.xga, ...), custom_call_target="tpu_custom_call" | custom-call | tf_op jit(solution)/shard_map/write_out/pallas_call | solution.py:470

commit v7 on v6

--- a/solution.py
+++ b/solution.py
@@ -23,9 +23,9 @@
 SCHEDULE = (
     ("xs", "cot"), ("xs", 4), ("xs", 3), ("ag", 0, 1, 1, 0), ("ag", 0, 0, 1, 1),
     ("ag", 0, 0, 1, 0), ("ag", 0, 1, 1, 1), ("xs", 5), ("ag", 0, 0, 2, 1), ("xs", 2), ("xs", 1),
-    ("xs", 6), ("xs", 0), ("ag", 0, 1, 2, 0), ("ag", 0, 1, 2, 1), ("ag", 0, 0, 2, 0),
+    ("xs", 6), ("ag", 0, 1, 2, 0), ("ag", 0, 1, 2, 1), ("ag", 0, 0, 2, 0), ("xs", 0),
     ("ag", 0, 0, 3, 1), ("g", 4), ("rs", 1, 0, 1), ("ag", 0, 1, 3, 1), ("rs", 0, 0, 0), ("g", 5),
-    ("rs", 1, 1, 1), ("xs", 7), ("wxB",), ("g", 3), ("rs", 0, 1, 1), ("use", 0, 7),
+    ("xs", 7), ("rs", 1, 1, 1), ("wxB",), ("g", 3), ("rs", 0, 1, 1), ("use", 0, 7),
     ("rs", 1, 1, 0), ("rs", 0, 1, 0), ("use", 0, 0), ("g", 2), ("g", 1), ("g", 6),
     ("rs", 0, 2, 1), ("rs", 1, 2, 1), ("px", 6), ("px", 5), ("rs", 1, 2, 0), ("rs", 0, 2, 0),
     ("g", 7), ("g", 0), ("rs", 0, 3, 1), ("px", 2), ("rs", 1, 3, 1), ("use", 0, 6),
@@ -36,8 +36,8 @@
     ("ag", 1, 0, 2, 0), ("px", 4), ("pk", 0), ("ex1", 0), ("ag", 1, 1, 2, 1), ("pk", 1),
     ("ag", 1, 0, 3, 1), ("ag", 1, 0, 3, 0), ("ag", 1, 1, 2, 0), ("ag", 0, 0, 4, 0),
     ("use", 1, 6), ("ag", 1, 1, 3, 1), ("use", 0, 3), ("ag", 1, 1, 3, 0), ("use", 0, 5),
-    ("use", 1, 1), ("ag", 1, 0, 4, 0), ("use", 0, 1), ("ag", 1, 1, 4, 1), ("use", 1, 5),
-    ("use", 0, 4), ("use", 1, 3), ("use", 1, 2),
+    ("use", 1, 1), ("use", 0, 1), ("ag", 1, 1, 4, 1), ("ag", 1, 0, 4, 0), ("use", 1, 2),
+    ("exf",), ("use", 1, 5), ("use", 0, 4), ("use", 1, 3),
 )
 
 
@@ -62,9 +62,9 @@
 
 
 def kernel(
-    act_h, w_h, cot_h, first_h, second_h, partner_h,
-    kvacc, xga, xgb, xgc, kvc, first_new, second_new, stepped, final, wg, aoth, ccat,
-    px_out, pk_out, pk_acc, acat, mom, rs_in, rs_out, gbuf, inbox_a, inbox_b, outbox, partner_s,
+    act_h, w_h, cot_h, first_h, second_h, partner_h, mix_h,
+    kvacc, xga, xgb, xgc, kvc, first_new, second_new, nwv, wg, aoth, ccat,
+    stepped, final, px_out, pk_out, pk_acc, acat, mom, rs_in, rs_out, gbuf, inbox_a, inbox_b, outbox, partner_s, mix_s,
     load_sem, act_sem, x_send, x_recv, wx_send, wx_recv, ag_send, ag_recv,
     rs_send, rs_recv, ex_send, ex_recv, px_send, px_recv, pk_send, pk_recv,
 ):
@@ -94,6 +94,7 @@
         "first": pltpu.make_async_copy(first_h, mom.at[0], load_sem.at[2]),
         "second": pltpu.make_async_copy(second_h, mom.at[1], load_sem.at[3]),
         "partner": pltpu.make_async_copy(partner_h, partner_s, load_sem.at[4]),
+        "mix": pltpu.make_async_copy(mix_h, mix_s, load_sem.at[5]),
     }
     for slot in range(NZ):
         loads[0, slot] = pltpu.make_async_copy(
@@ -290,6 +291,17 @@
             copy.start()
         final[part, rep] = outbox[part, rep]
 
+    def average():
+        loaded("mix")
+        mixing = mix_s[rep].astype(F32) / mix_denom
+        for part in range(2):
+            for copy in ex[1, part]:
+                copy.wait_recv()
+            own, other = stepped[part].astype(F32), final[part].astype(F32)
+            nwv[:, pl.ds(part * half, half)] = (
+                ((1.0 - mixing) * own + mixing * other).astype(BF).reshape(rows, half)
+            )
+
     barrier = pltpu.get_barrier_semaphore()
     others = [(lax.rem(rep + k, n_rep), me) for k in range(1, n_rep)]
     for device in (up, down, side, *others):
@@ -302,13 +314,13 @@
 
     actions = {
         "use": use_block, "g": product, "rs": reduce_send, "fin": finish,
-        "ex0": exchange_first, "ex1": exchange_second, "px": side_products, "pk": side_sum,
+        "ex0": exchange_first, "ex1": exchange_second, "px": side_products, "pk": side_sum, "exf": average,
     }
     for position, token in enumerate(SCHEDULE):
         if position == LATE_LOADS:
             for slot in range(NZ):
                 loads[1, slot].start()
-            for name in ("first", "second", "partner"):
+            for name in ("first", "second", "partner", "mix"):
                 loads[name].start()
         name = token[0]
         if name in actions:
@@ -322,19 +334,22 @@
                 arrived(("wxB",))
         copies[token].start()
 
-    for key, copy in copies.items():
-        arrived(key)
-        copy.wait_send()
-    for part in range(2):
-        for copy in ex[1, part]:
-            copy.wait_recv()
-        for phase in range(2):
+    for key in loads:
+        loaded(key)
+    for phase in range(2):
+        for part in range(2):
             for copy in ex[phase, part]:
                 copy.wait_send()
-    for key in loads:
-        loaded(key)
-
-
+    sent = [token for token in SCHEDULE if token in copies]
+    for token in sent[:-LAST]:
+        copies[token].wait_send()
+    for token in sent:
+        arrived(token)
+    for token in sent[-LAST:]:
+        copies[token].wait_send()
+
+
+LAST = 8
 LATE_LOADS = 16
 LEFT = tuple(
     (col, slot)
@@ -345,18 +360,16 @@
 
 
 def write_out(
-    kvacc, xga, xgb, xgc, kvc, first_new, second_new, stepped, final, wg, aoth, ccat, mix_h,
+    kvacc, xga, xgb, xgc, kvc, first_new, second_new, nwv, wg, aoth, ccat,
     kv_h, xg_h, nw_h, nf_h, ns_h,
-    kvb, xgl, nwv, mix_s, xg_sem, sem,
+    kvb, xgl, xg_sem, sem,
 ):
     tok = kvb.shape[0]
-    rows, cols = nwv.shape
-    half = cols // 2
-    mix_load = pltpu.make_async_copy(mix_h, mix_s, sem.at[4])
-    mix_load.start()
+    rows = nwv.shape[0]
     copies = [
         pltpu.make_async_copy(first_new, nf_h, sem.at[0]),
         pltpu.make_async_copy(second_new, ns_h, sem.at[1]),
+        pltpu.make_async_copy(nwv, nw_h, sem.at[3]),
     ]
     for slot in range(NZ):
         blocks = [(xga, 0, None, 0), (xgc, 1, 1, 2)]
@@ -385,16 +398,6 @@
     kvb[...] = total.astype(BF)
     copies.append(pltpu.make_async_copy(kvb, kv_h, sem.at[2]))
     copies[-1].start()
-    mix_load.wait()
-    mixing = mix_s[lax.axis_index("rep")].astype(F32) / mix_denom
-    for part in range(2):
-        nwv[:, pl.ds(part * half, half)] = (
-            ((1.0 - mixing) * stepped[part].astype(F32) + mixing * final[part].astype(F32))
-            .astype(BF)
-            .reshape(rows, half)
-        )
-    copies.append(pltpu.make_async_copy(nwv, nw_h, sem.at[3]))
-    copies[-1].start()
     for copy in copies:
         copy.wait()
 
@@ -424,15 +427,16 @@
             pltpu.VMEM((tok, cols), BF),
             pltpu.VMEM((rows, cols), F32),
             pltpu.VMEM((rows, cols), F32),
-            pltpu.VMEM(chunks, BF),
-            pltpu.VMEM(chunks, BF),
+            pltpu.VMEM((rows, cols), BF),
             pltpu.VMEM((2, NZ, rows, cols), BF),
             pltpu.VMEM((NZ, tok, rows // 2), BF),
             pltpu.VMEM((2 * tok, cols), BF),
         ),
-        in_specs=[hbm] * 6,
-        out_specs=[vmem] * 12,
+        in_specs=[hbm] * 7,
+        out_specs=[vmem] * 11,
         scratch_shapes=[
+            pltpu.VMEM(chunks, BF),
+            pltpu.VMEM(chunks, BF),
             pltpu.VMEM((NZ, tok, rows // 2), BF),
             pltpu.VMEM((tok, cols), BF),
             pltpu.VMEM((tok, cols), F32),
@@ -445,7 +449,8 @@
             pltpu.VMEM(chunks[1:], BF),
             pltpu.VMEM(chunks, BF),
             pltpu.SMEM((n_rep,), jnp.int32),
-            dma((5,)),
+            pltpu.SMEM((n_rep,), jnp.int32),
+            dma((6,)),
             dma((2, NZ)),
             dma((NZ + 1,)),
             dma((NZ + 1,)),
@@ -466,7 +471,12 @@
         compiler_params=pltpu.CompilerParams(
             collective_id=0, has_side_effects=True, vmem_limit_bytes=32 << 20
         ),
-    )(*(in_hbm(x) for x in (act, weights, cot, first_moment[0], second_moment[0], partner)))
+    )(
+        *(
+            in_hbm(x)
+            for x in (act, weights, cot, first_moment[0], second_moment[0], partner, mix_numerator)
+        )
+    )
     outs = pl.pallas_call(
         write_out,
         out_shape=(
@@ -476,19 +486,17 @@
             jax.ShapeDtypeStruct((rows, cols), F32),
             jax.ShapeDtypeStruct((rows, cols), F32),
         ),
-        in_specs=[vmem] * 12 + [hbm],
+        in_specs=[vmem] * 11,
         out_specs=[hbm] * 5,
         scratch_shapes=[
             pltpu.VMEM((tok, cols), BF),
             pltpu.VMEM((len(LEFT), tok, rows // 2), BF),
-            pltpu.VMEM((rows, cols), BF),
-            pltpu.SMEM((n_rep,), jnp.int32),
             dma((3, NZ)),
-            dma((5,)),
+            dma((4,)),
         ],
         name="write_out",
         compiler_params=pltpu.CompilerParams(vmem_limit_bytes=8 << 20),
-    )(*held, in_hbm(mix_numerator))
+    )(*held)
     return tuple(out[None] for out in outs)
 
 

time: 119 us -> 118 us (level)
  no operation moved by 1% of the time
where the time goes in v7:
time: 118 us
  Pallas kernels  117 us (99%)
    pallas_call x1, Pallas kernels, per_device(): pl.pallas_call(kernel, out_shape=(pltpu.VMEM((tok, cols), F32), pltpu.VME...  114 us
    pallas_call x1, Pallas kernels, per_device(): pl.pallas_call(write_out, out_shape=(jax.ShapeDtypeStruct((tok, cols), BF...  3.43 us

profile of v7, /device:TPU:1, one launch (start us, length us, event | category | flops | bytes accessed | tf_op | source)
XLA Modules:
  0.0 117.9 jit_solution(13876048637176371879)
XLA Ops:
  0.6 113.7 %step.1 = (f32[384,1024]{1,0:T(8,128)S(1)}, bf16[8,384,256]{2,1,0:T(8,128)(2,1)S(1)}, bf16[8,384,128]{2,1,0:T(8,128)(2,1)S(1)}, bf16[8,384,128]{2,1,0:T(8,128)(2...) custom-call(bf16[384,4096]{1,0:T(8,128)(2,1)} %bitcast.10, ...), custom_call_target="tpu_custom_call" | custom-call | tf_op jit(solution)/shard_map/step/pallas_call | solution.py:420
  114.3 3.4 %write_out.1 = (bf16[384,1024]{1,0:T(8,128)(2,1)}, bf16[384,4096]{1,0:T(8,128)(2,1)}, bf16[256,1024]{1,0:T(8,128)(2,1)}, f32[256,1024]{1,0:T(8,128)}, f32[256,1024]{1,0:T(8,128)}) custom-call(f32[384,1024]{1,0:T(8,128)S(1)} %get-tuple-element.21.kvacc, bf16[8,384,256]{2,1,0:T(8,128)(2,1)S(1)} %get-tuple-element.22.xga, ...), custom_call_target="tpu_custom_call" | custom-call | tf_op jit(solution)/shard_map/write_out/pallas_call | solution.py:480

commit v8 on v7

--- a/solution.py
+++ b/solution.py
@@ -21,9 +21,9 @@
 HOPS = NZ // 2
 
 SCHEDULE = (
-    ("xs", "cot"), ("xs", 4), ("xs", 3), ("ag", 0, 1, 1, 0), ("ag", 0, 0, 1, 1),
-    ("ag", 0, 0, 1, 0), ("ag", 0, 1, 1, 1), ("xs", 5), ("ag", 0, 0, 2, 1), ("xs", 2), ("xs", 1),
-    ("xs", 6), ("ag", 0, 1, 2, 0), ("ag", 0, 1, 2, 1), ("ag", 0, 0, 2, 0), ("xs", 0),
+    ("xs", "cot"), ("ag", 0, 1, 1, 0), ("ag", 0, 0, 1, 1), ("ag", 0, 0, 1, 0),
+    ("ag", 0, 1, 1, 1), ("xs", 4), ("xs", 3), ("xs", 5), ("ag", 0, 0, 2, 1), ("xs", 2),
+    ("xs", 1), ("xs", 6), ("ag", 0, 1, 2, 0), ("ag", 0, 1, 2, 1), ("ag", 0, 0, 2, 0), ("xs", 0),
     ("ag", 0, 0, 3, 1), ("g", 4), ("rs", 1, 0, 1), ("ag", 0, 1, 3, 1), ("rs", 0, 0, 0), ("g", 5),
     ("xs", 7), ("rs", 1, 1, 1), ("wxB",), ("g", 3), ("rs", 0, 1, 1), ("use", 0, 7),
     ("rs", 1, 1, 0), ("rs", 0, 1, 0), ("use", 0, 0), ("g", 2), ("g", 1), ("g", 6),
@@ -63,7 +63,7 @@
 
 def kernel(
     act_h, w_h, cot_h, first_h, second_h, partner_h, mix_h,
-    kvacc, xga, xgb, xgc, kvc, first_new, second_new, nwv, wg, aoth, ccat,
+    kvacc, xga, xgb, kvc, first_new, second_new, nwv, wg, aoth, ccat,
     stepped, final, px_out, pk_out, pk_acc, acat, mom, rs_in, rs_out, gbuf, inbox_a, inbox_b, outbox, partner_s, mix_s,
     load_sem, act_sem, x_send, x_recv, wx_send, wx_recv, ag_send, ag_recv,
     rs_send, rs_recv, ex_send, ex_recv, px_send, px_recv, pk_send, pk_recv,
@@ -101,7 +101,7 @@
             columns_of(act_h, 0, slot, rows), acat.at[slot, pl.ds(0, tok)], act_sem.at[0, slot]
         )
         loads[1, slot] = pltpu.make_async_copy(
-            columns_of(act_h, 1, slot, rows, 0), aoth.at[slot], act_sem.at[1, slot]
+            columns_of(act_h, 1, slot, rows), aoth.at[slot], act_sem.at[1, slot]
         )
     waited = set()
 
@@ -120,11 +120,11 @@
     }
     for slot in range(NZ):
         copies["xs", slot] = remote(
-            columns_of(act_h, 1, slot, rows), acat.at[slot, pl.ds(tok, tok)],
+            aoth.at[slot], acat.at[slot, pl.ds(tok, tok)],
             x_send.at[slot], x_recv.at[slot], side,
         )
         copies["px", slot] = remote(
-            px_out.at[slot], xgc.at[slot], px_send.at[slot], px_recv.at[slot], side
+            px_out.at[slot], xgb.at[slot, :, high_rows], px_send.at[slot], px_recv.at[slot], side
         )
     for part in range(2):
         span = (slice(None), pl.ds(part * half, half))
@@ -209,14 +209,18 @@
         if col == 0:
             tokens, block = acat[slot, pl.ds(0, tok)], wg[0, slot]
         else:
-            tokens, block = aoth[slot], wg[1, slot, low_rows]
+            tokens, block = aoth[slot, :, low_rows], wg[1, slot, low_rows]
         term = jnp.dot(tokens, block, preferred_element_type=F32)
         if used:
             kvacc[...] += term
         else:
             kvacc[...] = term
         used.append((col, slot))
-        (xga, xgb)[col][slot] = back_product(ccat[pl.ds(0, tok)], block)
+        back = back_product(ccat[pl.ds(0, tok)], block)
+        if col == 0:
+            xga[slot] = back
+        else:
+            xgb[slot, :, low_rows] = back
 
     sided = []
 
@@ -308,7 +312,10 @@
         pl.semaphore_signal(barrier, inc=1, device_id=device, device_id_type=MESH)
     loads["cot"].start()
     loads["w"].start()
-    for slot in (0, 7, 1, 4, 3, 5, 2, 6):
+    sends = [token[1] for token in SCHEDULE if token[0] == "xs" and token[1] != "cot"]
+    for slot in sends:
+        loads[1, slot].start()
+    for slot in sends:
         loads[0, slot].start()
     pl.semaphore_wait(barrier, 3 + n_rep - 1)
 
@@ -318,8 +325,6 @@
     }
     for position, token in enumerate(SCHEDULE):
         if position == LATE_LOADS:
-            for slot in range(NZ):
-                loads[1, slot].start()
             for name in ("first", "second", "partner", "mix"):
                 loads[name].start()
         name = token[0]
@@ -332,6 +337,8 @@
                 arrived(("ag", col, direction, hop - 1, part))
             elif col == 1:
                 arrived(("wxB",))
+        elif name == "xs" and token[1] != "cot":
+            loaded((1, token[1]))
         copies[token].start()
 
     for key in loads:
@@ -350,7 +357,7 @@
 
 
 LAST = 8
-LATE_LOADS = 16
+LATE_LOADS = 17
 LEFT = tuple(
     (col, slot)
     for slot in (0, 7, 1, 6, 2, 5, 3, 4)
@@ -360,7 +367,7 @@
 
 
 def write_out(
-    kvacc, xga, xgb, xgc, kvc, first_new, second_new, nwv, wg, aoth, ccat,
+    kvacc, xga, xgb, kvc, first_new, second_new, nwv, wg, aoth, ccat,
     kv_h, xg_h, nw_h, nf_h, ns_h,
     kvb, xgl, xg_sem, sem,
 ):
@@ -372,15 +379,15 @@
         pltpu.make_async_copy(nwv, nw_h, sem.at[3]),
     ]
     for slot in range(NZ):
-        blocks = [(xga, 0, None, 0), (xgc, 1, 1, 2)]
-        if (1, slot) not in LEFT:
-            blocks.append((xgb, 1, 0, 1))
-        for source, col, part, sem_row in blocks:
+        blocks = [(xga.at[slot], 0, None)]
+        if (1, slot) in LEFT:
+            blocks.append((xgb.at[slot, :, pl.ds(rows // 2, rows // 2)], 1, 1))
+        else:
+            blocks.append((xgb.at[slot], 1, None))
+        for source, col, part in blocks:
             copies.append(
                 pltpu.make_async_copy(
-                    source.at[slot],
-                    columns_of(xg_h, col, slot, rows, part),
-                    xg_sem.at[sem_row, slot],
+                    source, columns_of(xg_h, col, slot, rows, part), xg_sem.at[col, slot]
                 )
             )
     for copy in copies:
@@ -388,10 +395,10 @@
     total = kvacc[...] + kvc[...].astype(F32)
     for i, (col, slot) in enumerate(LEFT):
         block = wg[col, slot, pl.ds(0, rows // 2)]
-        total = total + jnp.dot(aoth[slot], block, preferred_element_type=F32)
+        total = total + jnp.dot(aoth[slot, :, pl.ds(0, rows // 2)], block, preferred_element_type=F32)
         xgl[i] = back_product(ccat[pl.ds(0, tok)], block)
         copy = pltpu.make_async_copy(
-            xgl.at[i], columns_of(xg_h, col, slot, rows, 0), xg_sem.at[col, slot]
+            xgl.at[i], columns_of(xg_h, col, slot, rows, 0), xg_sem.at[2, slot]
         )
         copy.start()
         copies.append(copy)
@@ -422,18 +429,17 @@
         out_shape=(
             pltpu.VMEM((tok, cols), F32),
             pltpu.VMEM((NZ, tok, rows), BF),
-            pltpu.VMEM((NZ, tok, rows // 2), BF),
-            pltpu.VMEM((NZ, tok, rows // 2), BF),
+            pltpu.VMEM((NZ, tok, rows), BF),
             pltpu.VMEM((tok, cols), BF),
             pltpu.VMEM((rows, cols), F32),
             pltpu.VMEM((rows, cols), F32),
             pltpu.VMEM((rows, cols), BF),
             pltpu.VMEM((2, NZ, rows, cols), BF),
-            pltpu.VMEM((NZ, tok, rows // 2), BF),
+            pltpu.VMEM((NZ, tok, rows), BF),
             pltpu.VMEM((2 * tok, cols), BF),
         ),
         in_specs=[hbm] * 7,
-        out_specs=[vmem] * 11,
+        out_specs=[vmem] * 10,
         scratch_shapes=[
             pltpu.VMEM(chunks, BF),
             pltpu.VMEM(chunks, BF),
@@ -486,7 +492,7 @@
             jax.ShapeDtypeStruct((rows, cols), F32),
             jax.ShapeDtypeStruct((rows, cols), F32),
         ),
-        in_specs=[vmem] * 11,
+        in_specs=[vmem] * 10,
         out_specs=[hbm] * 5,
         scratch_shapes=[
             pltpu.VMEM((tok, cols), BF),

time: 118 us -> 118 us (level)
  no operation moved by 1% of the time
where the time goes in v8:
time: 118 us
  Pallas kernels  117 us (99%)
    pallas_call x1, Pallas kernels, per_device(): pl.pallas_call(kernel, out_shape=(pltpu.VMEM((tok, cols), F32), pltpu.VME...  114 us
    pallas_call x1, Pallas kernels, per_device(): pl.pallas_call(write_out, out_shape=(jax.ShapeDtypeStruct((tok, cols), BF...  3.43 us

profile of v8, /device:TPU:1, one launch (start us, length us, event | category | flops | bytes accessed | tf_op | source)
XLA Modules:
  0.0 117.9 jit_solution(11570014547019076057)
XLA Ops:
  0.6 113.7 %step.1 = (f32[384,1024]{1,0:T(8,128)S(1)}, bf16[8,384,256]{2,1,0:T(8,128)(2,1)S(1)}, bf16[8,384,256]{2,1,0:T(8,128)(2,1)S(1)}, bf16[384,1024]{1,0:T(8,128)(2,1)...) custom-call(bf16[384,4096]{1,0:T(8,128)(2,1)} %bitcast.10, ...), custom_call_target="tpu_custom_call" | custom-call | tf_op jit(solution)/shard_map/step/pallas_call | solution.py:427
  114.3 3.4 %write_out.1 = (bf16[384,1024]{1,0:T(8,128)(2,1)}, bf16[384,4096]{1,0:T(8,128)(2,1)}, bf16[256,1024]{1,0:T(8,128)(2,1)}, f32[256,1024]{1,0:T(8,128)}, f32[256,1024]{1,0:T(8,128)}) custom-call(f32[384,1024]{1,0:T(8,128)S(1)} %get-tuple-element.20.kvacc, bf16[8,384,256]{2,1,0:T(8,128)(2,1)S(1)} %get-tuple-element.21.xga, ...), custom_call_target="tpu_custom_call" | custom-call | tf_op jit(solution)/shard_map/write_out/pallas_call | solution.py:486

commit v9 on v8

--- a/solution.py
+++ b/solution.py
@@ -310,13 +310,7 @@
     others = [(lax.rem(rep + k, n_rep), me) for k in range(1, n_rep)]
     for device in (up, down, side, *others):
         pl.semaphore_signal(barrier, inc=1, device_id=device, device_id_type=MESH)
-    loads["cot"].start()
-    loads["w"].start()
     sends = [token[1] for token in SCHEDULE if token[0] == "xs" and token[1] != "cot"]
-    for slot in sends:
-        loads[1, slot].start()
-    for slot in sends:
-        loads[0, slot].start()
     pl.semaphore_wait(barrier, 3 + n_rep - 1)
 
     actions = {
@@ -324,6 +318,11 @@
         "ex0": exchange_first, "ex1": exchange_second, "px": side_products, "pk": side_sum, "exf": average,
     }
     for position, token in enumerate(SCHEDULE):
+        if position == FIRST_LOADS:
+            for slot in sends:
+                loads[1, slot].start()
+            for key in ("cot", "w", *((0, slot) for slot in sends)):
+                loads[key].start()
         if position == LATE_LOADS:
             for name in ("first", "second", "partner", "mix"):
                 loads[name].start()
@@ -357,6 +356,7 @@
 
 
 LAST = 8
+FIRST_LOADS = 5
 LATE_LOADS = 17
 LEFT = tuple(
     (col, slot)

time: 118 us -> 118 us (level)
  no operation moved by 1% of the time
where the time goes in v9:
time: 118 us
  Pallas kernels  117 us (99%)
    pallas_call x1, Pallas kernels, per_device(): pl.pallas_call(kernel, out_shape=(pltpu.VMEM((tok, cols), F32), pltpu.VME...  114 us
    pallas_call x1, Pallas kernels, per_device(): pl.pallas_call(write_out, out_shape=(jax.ShapeDtypeStruct((tok, cols), BF...  3.43 us

profile of v9, /device:TPU:1, one launch (start us, length us, event | category | flops | bytes accessed | tf_op | source)
XLA Modules:
  0.0 117.9 jit_solution(3256768324697273079)
XLA Ops:
  0.6 113.7 %step.1 = (f32[384,1024]{1,0:T(8,128)S(1)}, bf16[8,384,256]{2,1,0:T(8,128)(2,1)S(1)}, bf16[8,384,256]{2,1,0:T(8,128)(2,1)S(1)}, bf16[384,1024]{1,0:T(8,128)(2,1)...) custom-call(bf16[384,4096]{1,0:T(8,128)(2,1)} %bitcast.10, ...), custom_call_target="tpu_custom_call" | custom-call | tf_op jit(solution)/shard_map/step/pallas_call | solution.py:427
  114.3 3.4 %write_out.1 = (bf16[384,1024]{1,0:T(8,128)(2,1)}, bf16[384,4096]{1,0:T(8,128)(2,1)}, bf16[256,1024]{1,0:T(8,128)(2,1)}, f32[256,1024]{1,0:T(8,128)}, f32[256,1024]{1,0:T(8,128)}) custom-call(f32[384,1024]{1,0:T(8,128)S(1)} %get-tuple-element.20.kvacc, bf16[8,384,256]{2,1,0:T(8,128)(2,1)S(1)} %get-tuple-element.21.xga, ...), custom_call_target="tpu_custom_call" | custom-call | tf_op jit(solution)/shard_map/write_out/pallas_call | solution.py:486
